TPU v7x, 32 devices: a whole 2x2x4 slice. The times are simulated.
32 devices in a mesh: rep: 4 (over y, core), fsdp: 8 (over z, x).
Axes of the slice: x: 2, y: 2, z: 4, core: 2. Of those that a mesh axis runs over, the one named last changes fastest.
Arguments:
- visual: bfloat16 [32, 128, 768], P(('rep', 'fsdp')), may hold values from -6 to 6
- text: bfloat16 [32, 1280, 768], P(('rep', 'fsdp')), may hold values from -6 to 6
- visual_valid: int32 [32, 128], P(('rep', 'fsdp')), may hold values from 0 to 1, as said below
- block_owner: int32 [32, 1280], P(('rep', 'fsdp')), may hold values from 0 to 127, as said below
- cross_query: bfloat16 [768, 768], P('fsdp'), may hold values from -0.21875 to 0.21875
- cross_keyval: bfloat16 [768, 1536], P('fsdp'), may hold values from -0.21875 to 0.21875
- cross_output: bfloat16 [768, 768], P('fsdp'), may hold values from -0.625 to 0.625
- gate_weight: bfloat16 [1536, 768], P('fsdp'), may hold values from -0.15625 to 0.15625
- self_qkv: bfloat16 [768, 2304], P('fsdp'), may hold values from -0.21875 to 0.21875
- self_output: bfloat16 [768, 768], P('fsdp'), may hold values from -0.875 to 0.875
- ffn_up: bfloat16 [768, 3072], P('fsdp'), may hold values from -0.21875 to 0.21875
- ffn_down: bfloat16 [3072, 768], P('fsdp'), may hold values from -0.109375 to 0.109375
- norm_gains: float32 [3072], P('fsdp'), may hold values from 0.5 to 1.5
- norm_biases: float32 [3072], P('fsdp'), may hold values from -1.8 to 1.8
- cotangent: bfloat16 [32, 128, 768], P(('rep', 'fsdp')), may hold values from -6 to 6
Outputs:
- layer_out: bfloat16 [32, 128, 768], P(('rep', 'fsdp'))
- grad_visual: float32 [32, 128, 768], P(('rep', 'fsdp'))
- grad_text: float32 [32, 1280, 768], P(('rep', 'fsdp'))
- grad_cross_query: float32 [768, 768], P('fsdp')
- grad_cross_keyval: float32 [768, 1536], P('fsdp')
- grad_cross_output: float32 [768, 768], P('fsdp')
- grad_gate_weight: float32 [1536, 768], P('fsdp')
- grad_self_qkv: float32 [768, 2304], P('fsdp')
- grad_self_output: float32 [768, 768], P('fsdp')
- grad_ffn_up: float32 [768, 3072], P('fsdp')
- grad_ffn_down: float32 [3072, 768], P('fsdp')
- grad_norm_gains: float32 [3072], P('fsdp')
- grad_norm_biases: float32 [3072], P('fsdp')
Inputs may be any that keep to these rules, and one draw needn't show every extreme that they name: `visual_valid`: in every page the real visual blocks come first and the padded ones last; each page has at least a quarter of 128 real blocks and at least one padded block. `block_owner`: each visual block of a page owns exactly 10 of that page's text blocks.
All inputs are finite; a program needn't handle non-finite values.
Results may differ from a plain program's by a relative error of at most 0.04.
Values may be sent and summed in bfloat16 or wider, within the bound.
No kernel may reach another device: no remote copies, remote signals or barrier semaphores. Data moves between devices by JAX's collectives and lax.ppermute only.
A program may use at most 192 MiB of HBM per device.

v0:
```python
import jax
import jax.numpy as jnp
from jax import lax
from jax.sharding import PartitionSpec as P

H = 12
HD = 64


epsilon = 1e-05
filtered_logits = -1000000000.0
shared_sheet_reward = 6.0
highest = lax.Precision.HIGHEST


def layer_norm(inputs, gain_row, bias_row):
    row_mean = jnp.mean(inputs, -1, keepdims=True)
    centred = inputs - row_mean
    factor = lax.rsqrt(jnp.mean(centred * centred, -1, keepdims=True) + epsilon)
    normal = centred * factor
    return (normal * gain_row + bias_row, normal, factor)


def norm_back(gradient, normal, factor, gain_row):
    scaled = gradient * gain_row
    centred_grad = (
        scaled
        - jnp.mean(scaled, -1, keepdims=True)
        - normal * jnp.mean(scaled * normal, -1, keepdims=True)
    )
    return (centred_grad * factor, jnp.sum(gradient * normal, (0, 1)), jnp.sum(gradient, (0, 1)))


def project(inputs, weight):
    return jnp.einsum("pvd,de->pve", inputs, weight, preferred_element_type=jnp.float32)


def project_back(gradient, weight):
    return jnp.einsum("pve,de->pvd", gradient, weight, preferred_element_type=jnp.float32)


def weight_grad(inputs, gradient):
    return jnp.einsum("pvd,pve->de", inputs, gradient, preferred_element_type=jnp.float32)


def split_heads(inputs):
    return inputs.reshape(inputs.shape[0], inputs.shape[1], H, HD)


def page_scores(queries, key_rows, score_bias):
    raw_scores = jnp.einsum("qhe,khe->hqk", queries, key_rows, preferred_element_type=jnp.float32)
    return raw_scores * queries.shape[-1] ** (-0.5) + score_bias[None]


def attend_page(page_items):
    queries, key_rows, value_rows, score_bias = page_items
    scores = page_scores(queries, key_rows, score_bias)
    peak_score = jnp.max(scores, -1, keepdims=True)
    exponent = jnp.exp(scores - peak_score)
    expo_total = jnp.sum(exponent, -1, keepdims=True)
    weighting = (exponent / expo_total).astype(jnp.bfloat16)
    mixed_rows = jnp.einsum(
        "hqk,khe->qhe", weighting, value_rows, preferred_element_type=jnp.float32
    )
    return (mixed_rows.reshape(mixed_rows.shape[0], -1), peak_score + jnp.log(expo_total))


def attend_page_back(page_items):
    grad_mixed, queries, key_rows, value_rows, score_bias, log_total = page_items
    grad_heads = grad_mixed.reshape(grad_mixed.shape[0], H, HD)
    scaling = queries.shape[-1] ** (-0.5)
    weighting = jnp.exp(page_scores(queries, key_rows, score_bias) - log_total)
    grad_values = jnp.einsum(
        "hqk,qhe->khe",
        weighting.astype(jnp.bfloat16),
        grad_heads,
        preferred_element_type=jnp.float32,
    )
    grad_weighting = jnp.einsum(
        "qhe,khe->hqk", grad_heads, value_rows, preferred_element_type=jnp.float32
    )
    inner_sum = jnp.sum(weighting * grad_weighting, -1, keepdims=True)
    grad_scores = weighting * (grad_weighting - inner_sum)
    grad_queries = (
        jnp.einsum("hqk,khe->qhe", grad_scores, key_rows.astype(jnp.float32), precision=highest)
        * scaling
    )
    grad_keys = (
        jnp.einsum("hqk,qhe->khe", grad_scores, queries.astype(jnp.float32), precision=highest)
        * scaling
    )
    return (
        grad_queries.reshape(grad_queries.shape[0], -1),
        grad_keys.reshape(grad_keys.shape[0], -1),
        grad_values.reshape(grad_values.shape[0], -1),
    )


def local(
    visual,
    text,
    visual_valid,
    block_owner,
    cross_query,
    cross_keyval,
    cross_output,
    gate_weight,
    self_qkv,
    self_output,
    ffn_up,
    ffn_down,
    norm_gains,
    norm_biases,
    cotangent,
):
    shards = (
        cross_query,
        cross_keyval,
        cross_output,
        gate_weight,
        self_qkv,
        self_output,
        ffn_up,
        ffn_down,
        norm_gains,
        norm_biases,
    )
    gathered = (
        lax.all_gather(shards[0], "fsdp", axis=0, tiled=True),
        lax.all_gather(shards[1], "fsdp", axis=0, tiled=True),
        lax.all_gather(shards[2], "fsdp", axis=0, tiled=True),
        lax.all_gather(shards[3], "fsdp", axis=0, tiled=True),
        lax.all_gather(shards[4], "fsdp", axis=0, tiled=True),
        lax.all_gather(shards[5], "fsdp", axis=0, tiled=True),
        lax.all_gather(shards[6], "fsdp", axis=0, tiled=True),
        lax.all_gather(shards[7], "fsdp", axis=0, tiled=True),
        lax.all_gather(shards[8].astype(jnp.bfloat16), "fsdp", axis=0, tiled=True).astype(
            jnp.float32
        ),
        lax.all_gather(shards[9].astype(jnp.bfloat16), "fsdp", axis=0, tiled=True).astype(
            jnp.float32
        ),
    )
    model_width = visual.shape[-1]
    page_count, visual_count = (visual.shape[0], visual.shape[1])
    gain_rows = gathered[8].reshape(4, model_width)
    biases = gathered[9].reshape(4, model_width)
    visual_rows = visual.astype(jnp.float32)
    normed_full, normal_one, factor_one = layer_norm(visual_rows, gain_rows[0], biases[0])
    normed = normed_full.astype(jnp.bfloat16)
    text_full, normal_text, factor_text = layer_norm(
        text.astype(jnp.float32), gain_rows[1], biases[1]
    )
    text_normed = text_full.astype(jnp.bfloat16)
    queries = split_heads(project(normed, gathered[0]).astype(jnp.bfloat16))
    keyval = project(text_normed, gathered[1]).astype(jnp.bfloat16)
    key_heads = split_heads(keyval[..., :model_width])
    value_heads = split_heads(keyval[..., model_width:])
    word_locations = lax.broadcasted_iota(jnp.int32, (1, visual_count, 1), 1)
    parent_sheet = block_owner[:, None, :] == word_locations
    word_unit_present = jnp.sum(jnp.where(parent_sheet, visual_valid[:, :, None], 0), axis=1) > 0
    mixed_sense_offset = (
        jnp.where(parent_sheet, shared_sheet_reward, 0.0)
        + jnp.where(word_unit_present, 0.0, filtered_logits)[:, None, :]
    )
    mixed_full, cross_log = lax.map(
        attend_page, (queries, key_heads, value_heads, mixed_sense_offset)
    )
    mixed_rows = mixed_full.astype(jnp.bfloat16)
    cross_rows = project(mixed_rows, gathered[2]).astype(jnp.bfloat16)
    cross_full = cross_rows.astype(jnp.float32)
    gate_rows = jax.nn.sigmoid(
        project(normed, gathered[3][:model_width]) + project(cross_rows, gathered[3][model_width:])
    )
    joined_rows = visual_rows + gate_rows * cross_full
    second_full, normal_two, factor_two = layer_norm(joined_rows, gain_rows[2], biases[2])
    second = second_full.astype(jnp.bfloat16)
    triple = project(second, gathered[4]).astype(jnp.bfloat16)
    self_queries = split_heads(triple[..., :model_width])
    self_keys = split_heads(triple[..., model_width : 2 * model_width])
    self_values = split_heads(triple[..., 2 * model_width :])
    self_bias = jnp.broadcast_to(
        jnp.where(visual_valid > 0, 0.0, filtered_logits)[:, None, :],
        (page_count, visual_count, visual_count),
    )
    attended_full, self_log = lax.map(
        attend_page, (self_queries, self_keys, self_values, self_bias)
    )
    attended = attended_full.astype(jnp.bfloat16)
    carried = joined_rows + project(attended, gathered[5])
    third_full, normal_three, factor_three = layer_norm(carried, gain_rows[3], biases[3])
    third_rows = third_full.astype(jnp.bfloat16)
    lifted = project(third_rows, gathered[6])
    active_full, gelu_pullback = jax.vjp(
        lambda inputs: jax.nn.gelu(inputs, approximate=True), lifted
    )
    active = active_full.astype(jnp.bfloat16)
    layer_out = (carried + project(active, gathered[7])).astype(jnp.bfloat16)
    weights_back = (
        lax.all_gather(shards[0], "fsdp", axis=0, tiled=True),
        lax.all_gather(shards[1], "fsdp", axis=0, tiled=True),
        lax.all_gather(shards[2], "fsdp", axis=0, tiled=True),
        lax.all_gather(shards[3], "fsdp", axis=0, tiled=True),
        lax.all_gather(shards[4], "fsdp", axis=0, tiled=True),
        lax.all_gather(shards[5], "fsdp", axis=0, tiled=True),
        lax.all_gather(shards[6], "fsdp", axis=0, tiled=True),
        lax.all_gather(shards[7], "fsdp", axis=0, tiled=True),
        lax.all_gather(shards[8].astype(jnp.bfloat16), "fsdp", axis=0, tiled=True).astype(
            jnp.float32
        ),
        lax.all_gather(shards[9].astype(jnp.bfloat16), "fsdp", axis=0, tiled=True).astype(
            jnp.float32
        ),
    )
    grad_ffn_down = weight_grad(active, cotangent)
    grad_lifted = gelu_pullback(project_back(cotangent, weights_back[7]))[0].astype(jnp.bfloat16)
    grad_ffn_up = weight_grad(third_rows, grad_lifted)
    back_three, gain_three, bias_three = norm_back(
        project_back(grad_lifted, weights_back[6]), normal_three, factor_three, gain_rows[3]
    )
    grad_carried = cotangent.astype(jnp.float32) + back_three
    carried_low = grad_carried.astype(jnp.bfloat16)
    grad_self_output = weight_grad(attended, carried_low)
    grad_attended = project_back(carried_low, weights_back[5]).astype(jnp.bfloat16)
    self_grads = lax.map(
        attend_page_back, (grad_attended, self_queries, self_keys, self_values, self_bias, self_log)
    )
    grad_triple = jnp.concatenate(self_grads, -1).astype(jnp.bfloat16)
    grad_self_qkv = weight_grad(second, grad_triple)
    back_two, gain_two, bias_two = norm_back(
        project_back(grad_triple, weights_back[4]), normal_two, factor_two, gain_rows[2]
    )
    grad_joined = grad_carried + back_two
    grad_gate_in = (grad_joined * cross_full * gate_rows * (1.0 - gate_rows)).astype(jnp.bfloat16)
    grad_gate_weight = jnp.concatenate(
        [weight_grad(normed, grad_gate_in), weight_grad(cross_rows, grad_gate_in)], 0
    )
    grad_cross = (
        grad_joined * gate_rows + project_back(grad_gate_in, weights_back[3][model_width:])
    ).astype(jnp.bfloat16)
    grad_cross_output = weight_grad(mixed_rows, grad_cross)
    grad_mixed = project_back(grad_cross, weights_back[2]).astype(jnp.bfloat16)
    cross_query_grad, cross_key_grad, cross_value_grad = lax.map(
        attend_page_back,
        (grad_mixed, queries, key_heads, value_heads, mixed_sense_offset, cross_log),
    )
    queries_low = cross_query_grad.astype(jnp.bfloat16)
    grad_cross_query = weight_grad(normed, queries_low)
    grad_normed = project_back(grad_gate_in, weights_back[3][:model_width]) + project_back(
        queries_low, weights_back[0]
    )
    keyval_low = jnp.concatenate([cross_key_grad, cross_value_grad], -1).astype(jnp.bfloat16)
    grad_cross_keyval = weight_grad(text_normed, keyval_low)
    back_one, gain_one, bias_one = norm_back(grad_normed, normal_one, factor_one, gain_rows[0])
    grad_visual = grad_joined + back_one
    grad_text, gain_text, bias_text = norm_back(
        project_back(keyval_low, weights_back[1]), normal_text, factor_text, gain_rows[1]
    )
    gradients = (
        grad_cross_query,
        grad_cross_keyval,
        grad_cross_output,
        grad_gate_weight,
        grad_self_qkv,
        grad_self_output,
        grad_ffn_up,
        grad_ffn_down,
        jnp.concatenate([gain_one, gain_text, gain_two, gain_three]),
        jnp.concatenate([bias_one, bias_text, bias_two, bias_three]),
    )
    shares = (
        lax.psum_scatter(
            gradients[0].astype(jnp.bfloat16), "fsdp", scatter_dimension=0, tiled=True
        ).astype(jnp.float32),
        lax.psum_scatter(
            gradients[1].astype(jnp.bfloat16), "fsdp", scatter_dimension=0, tiled=True
        ).astype(jnp.float32),
        lax.psum_scatter(
            gradients[2].astype(jnp.bfloat16), "fsdp", scatter_dimension=0, tiled=True
        ).astype(jnp.float32),
        lax.psum_scatter(
            gradients[3].astype(jnp.bfloat16), "fsdp", scatter_dimension=0, tiled=True
        ).astype(jnp.float32),
        lax.psum_scatter(
            gradients[4].astype(jnp.bfloat16), "fsdp", scatter_dimension=0, tiled=True
        ).astype(jnp.float32),
        lax.psum_scatter(
            gradients[5].astype(jnp.bfloat16), "fsdp", scatter_dimension=0, tiled=True
        ).astype(jnp.float32),
        lax.psum_scatter(
            gradients[6].astype(jnp.bfloat16), "fsdp", scatter_dimension=0, tiled=True
        ).astype(jnp.float32),
        lax.psum_scatter(
            gradients[7].astype(jnp.bfloat16), "fsdp", scatter_dimension=0, tiled=True
        ).astype(jnp.float32),
        lax.psum_scatter(
            gradients[8].astype(jnp.bfloat16), "fsdp", scatter_dimension=0, tiled=True
        ).astype(jnp.float32),
        lax.psum_scatter(
            gradients[9].astype(jnp.bfloat16), "fsdp", scatter_dimension=0, tiled=True
        ).astype(jnp.float32),
    )
    totals = (
        lax.psum(shares[0].astype(jnp.bfloat16), "rep").astype(jnp.float32),
        lax.psum(shares[1].astype(jnp.bfloat16), "rep").astype(jnp.float32),
        lax.psum(shares[2].astype(jnp.bfloat16), "rep").astype(jnp.float32),
        lax.psum(shares[3].astype(jnp.bfloat16), "rep").astype(jnp.float32),
        lax.psum(shares[4].astype(jnp.bfloat16), "rep").astype(jnp.float32),
        lax.psum(shares[5].astype(jnp.bfloat16), "rep").astype(jnp.float32),
        lax.psum(shares[6].astype(jnp.bfloat16), "rep").astype(jnp.float32),
        lax.psum(shares[7].astype(jnp.bfloat16), "rep").astype(jnp.float32),
        lax.psum(shares[8].astype(jnp.bfloat16), "rep").astype(jnp.float32),
        lax.psum(shares[9].astype(jnp.bfloat16), "rep").astype(jnp.float32),
    )
    return (
        layer_out,
        grad_visual,
        grad_text,
        totals[0],
        totals[1],
        totals[2],
        totals[3],
        totals[4],
        totals[5],
        totals[6],
        totals[7],
        totals[8],
        totals[9],
    )


def solution(mesh):
    in_specs = (
        P(("rep", "fsdp"), None, None),
        P(("rep", "fsdp"), None, None),
        P(("rep", "fsdp"), None),
        P(("rep", "fsdp"), None),
        P("fsdp", None),
        P("fsdp", None),
        P("fsdp", None),
        P("fsdp", None),
        P("fsdp", None),
        P("fsdp", None),
        P("fsdp", None),
        P("fsdp", None),
        P("fsdp"),
        P("fsdp"),
        P(("rep", "fsdp"), None, None),
    )
    out_specs = (
        P(("rep", "fsdp"), None, None),
        P(("rep", "fsdp"), None, None),
        P(("rep", "fsdp"), None, None),
        P("fsdp", None),
        P("fsdp", None),
        P("fsdp", None),
        P("fsdp", None),
        P("fsdp", None),
        P("fsdp", None),
        P("fsdp", None),
        P("fsdp", None),
        P("fsdp"),
        P("fsdp"),
    )
    return jax.shard_map(local, mesh=mesh, in_specs=in_specs, out_specs=out_specs, check_vma=False)
```

profile of v0, /device:TPU:1, one launch (start us, length us, event | category | flops | bytes accessed | tf_op | source)
XLA Modules:
  0.0 1184.3 jit_solution(11605284644913402647)
XLA Ops:
  14.5 22.9 %all-gather.1 = bf16[8,1,384]{2,1,0:T(2,128)(2,1)S(1)} all-gather(bf16[1,1,384]{2,1,0:T(2,128)(2,1)S(1)} %reshape.626), channel_id=1, replica_groups=mesh['rep'=4,'fsdp'=8] {'fsdp'}, dimensions={0}, use_global_device_ids=true | all-gather | bytes 6912 | tf_op jit(solution)/shard_map/all_gather | solution.py:140
  38.1 22.0 %all-gather = bf16[8,1,384]{2,1,0:T(2,128)(2,1)S(1)} all-gather(bf16[1,1,384]{2,1,0:T(2,128)(2,1)S(1)} %reshape.624), channel_id=1, replica_groups=mesh['rep'=4,'fsdp'=8] {'fsdp'}, dimensions={0}, use_global_device_ids=true | all-gather | bytes 6912 | tf_op jit(solution)/shard_map/all_gather | solution.py:137
  62.2 43.2 %all-gather.13.cloned.1.call-done = bf16[768,1536]{1,0:T(8,128)(2,1)} async-done(((bf16[96,1536]{1,0:T(8,128)(2,1)}), bf16[768,1536]{1,0:T(8,128)(2,1)}) %all-gather.13.cloned.1.call-update) | async-done | bytes 2359312 | tf_op jit(solution)/shard_map/all_gather | solution.py:130
  105.4 5.5 fusion.1
  129.6 17.6 %all-gather.17.cloned.1.call-done = bf16[768,768]{1,0:T(8,128)(2,1)} async-done(((bf16[96,768]{1,0:T(8,128)(2,1)}), bf16[768,768]{1,0:T(8,128)(2,1)}) %all-gather.17.cloned.1.call-update) | async-done | bytes 1179664 | tf_op jit(solution)/shard_map/all_gather | solution.py:131
  148.8 51.3 %all-gather.11.cloned.1.call-done = bf16[1536,768]{1,0:T(8,128)(2,1)} async-done(((bf16[192,768]{1,0:T(8,128)(2,1)}), bf16[1536,768]{1,0:T(8,128)(2,1)}) %all-gather.11.cloned.1.call-update) | async-done | bytes 2359312 | tf_op jit(solution)/shard_map/all_gather | solution.py:132
  204.4 61.7 %all-gather.19.cloned.1.call-done = bf16[768,2304]{1,0:T(8,128)(2,1)} async-done(((bf16[96,2304]{1,0:T(8,128)(2,1)}), bf16[768,2304]{1,0:T(8,128)(2,1)}) %all-gather.19.cloned.1.call-update) | async-done | bytes 3538960 | tf_op jit(solution)/shard_map/all_gather | solution.py:133
  273.0 34.5 %all-gather.21.cloned.1.call-done = bf16[768,768]{1,0:T(8,128)(2,1)} async-done(((bf16[96,768]{1,0:T(8,128)(2,1)}), bf16[768,768]{1,0:T(8,128)(2,1)}) %all-gather.21.cloned.1.call-update) | async-done | bytes 1179664 | tf_op jit(solution)/shard_map/all_gather | solution.py:134
  310.4 78.2 %all-gather.23.cloned.1.call-done = bf16[768,3072]{1,0:T(8,128)(2,1)} async-done(((bf16[96,3072]{1,0:T(8,128)(2,1)}), bf16[768,3072]{1,0:T(8,128)(2,1)}) %all-gather.23.cloned.1.call-update) | async-done | bytes 4718608 | tf_op jit(solution)/shard_map/all_gather | solution.py:135
  393.0 75.9 %all-gather.25.cloned.1.call-done = bf16[3072,768]{1,0:T(8,128)(2,1)} async-done(((bf16[384,768]{1,0:T(8,128)(2,1)}), bf16[3072,768]{1,0:T(8,128)(2,1)}) %all-gather.25.cloned.1.call-update) | async-done | bytes 4718608 | tf_op jit(solution)/shard_map/all_gather | solution.py:136
  493.9 12.2 %reduce-scatter.9.cloned.1.call-start = ((), (), s32[]{:S(2)}) async-start(), calls=%async_computation.16 | async-start | bytes 1327104 | tf_op jit(solution)/shard_map/reduce_scatter | solution.py:272
  510.5 6.0 multiply_reduce_fusion
  517.3 6.2 fusion.44
  535.4 11.3 fusion.24
  575.6 6.0 fusion.14
  584.1 28.2 %all-reduce.2 = (bf16[3072]{0:T(1024)(128)(2,1)S(1)}, bf16[3072]{0:T(1024)(128)(2,1)S(1)}) all-reduce(bf16[3072]{0:T(1024)(128)(2,1)S(1)} %pad_maximum_fusion.7, bf16[3072]{0:T(1024)(128)(2,1)S(1)} %pad_maximum_fusion.8), channel_id=10, replica_groups=mesh['rep'=4,'fsdp'=8] {'fsdp'}, use_global_device_ids=true, to_apply=%region_43.44.clone | all-reduce | flops 6144 | bytes 24576
  612.5 12.8 %all-reduce.3 = (bf16[384]{0:T(512)(128)(2,1)S(1)}, bf16[384]{0:T(512)(128)(2,1)S(1)}) all-reduce(bf16[384]{0:T(512)(128)(2,1)S(1)} %dynamic-slice.3, bf16[384]{0:T(512)(128)(2,1)S(1)} %dynamic-slice.5), channel_id=1, replica_groups=mesh['rep'=4,'fsdp'=8] {'rep'}, use_global_device_ids=true, to_apply=%region_44.45 | all-reduce | flops 768 | bytes 3072 | tf_op jit(solution)/shard_map/psum | solution.py:312
  627.5 51.8 %reduce-scatter.9.cloned.1.call-done = bf16[96,768]{1,0:T(8,128)(2,1)} async-done(((bf16[768,768]{1,0:T(8,128)(2,1)}), bf16[96,768]{1,0:T(8,128)(2,1)}) %reduce-scatter.9.cloned.1.call-update) | async-done | bytes 147472 | tf_op jit(solution)/shard_map/reduce_scatter | solution.py:272
  679.3 72.0 %reduce-scatter.15.cloned.1.call-done = bf16[192,768]{1,0:T(8,128)(2,1)} async-done(((bf16[1536,768]{1,0:T(8,128)(2,1)}), bf16[192,768]{1,0:T(8,128)(2,1)}) %reduce-scatter.15.cloned.1.call-update) | async-done | bytes 294928 | tf_op jit(solution)/shard_map/reduce_scatter | solution.py:281
  751.2 71.5 %reduce-scatter.11.cloned.1.call-done = bf16[96,1536]{1,0:T(8,128)(2,1)} async-done(((bf16[768,1536]{1,0:T(8,128)(2,1)}), bf16[96,1536]{1,0:T(8,128)(2,1)}) %reduce-scatter.11.cloned.1.call-update) | async-done | bytes 294928 | tf_op jit(solution)/shard_map/reduce_scatter | solution.py:275
  822.8 82.5 %reduce-scatter.17.cloned.1.call-done = bf16[96,2304]{1,0:T(8,128)(2,1)} async-done(((bf16[768,2304]{1,0:T(8,128)(2,1)}), bf16[96,2304]{1,0:T(8,128)(2,1)}) %reduce-scatter.17.cloned.1.call-update) | async-done | bytes 442384 | tf_op jit(solution)/shard_map/reduce_scatter | solution.py:284
  905.2 98.6 %reduce-scatter.23.cloned.1.call-done = bf16[384,768]{1,0:T(8,128)(2,1)} async-done(((bf16[3072,768]{1,0:T(8,128)(2,1)}), bf16[384,768]{1,0:T(8,128)(2,1)}) %reduce-scatter.23.cloned.1.call-update) | async-done | bytes 589840 | tf_op jit(solution)/shard_map/reduce_scatter | solution.py:293
  1003.8 98.6 %reduce-scatter.21.cloned.1.call-done = bf16[96,3072]{1,0:T(8,128)(2,1)} async-done(((bf16[768,3072]{1,0:T(8,128)(2,1)}), bf16[96,3072]{1,0:T(8,128)(2,1)}) %reduce-scatter.21.cloned.1.call-update) | async-done | bytes 589840 | tf_op jit(solution)/shard_map/reduce_scatter | solution.py:290
  1109.8 56.6 %all-reduce.7.cloned.1.call-done = (bf16[96,768]{1,0:T(8,128)(2,1)}, bf16[96,1536]{1,0:T(8,128)(2,1)}, bf16[96,768]{1,0:T(8,128)(2,1)}, bf16[192,768]{1,0:T(8,12...) async-done(((bf16[96,768]{1,0:T(8,128)(2,1)}, bf16[96,1536]{1,0:T(8,128)(2,1)}, ...) | async-done | bytes 2654224 | tf_op jit(solution)/shard_map/psum | solution.py:304
  (343 shorter events, 140.9 us)
Async XLA Ops:
  7.2 53.1 %all-gather.15.cloned.1.call-start = ((), (), s32[]{:S(2)}) async-start(), calls=%async_computation.10 | async-start | bytes 1327104 | tf_op jit(solution)/shard_map/all_gather | solution.py:129
  8.0 97.4 %all-gather.13.cloned.1.call-start = ((), (), s32[]{:S(2)}) async-start(), calls=%async_computation.9 | async-start | bytes 2654208 | tf_op jit(solution)/shard_map/all_gather | solution.py:130
  8.7 138.4 %all-gather.17.cloned.1.call-start = ((), (), s32[]{:S(2)}) async-start(), calls=%async_computation.11 | async-start | bytes 1327104 | tf_op jit(solution)/shard_map/all_gather | solution.py:131
  9.5 190.7 %all-gather.11.cloned.1.call-start = ((), (), s32[]{:S(2)}) async-start(), calls=%async_computation.8 | async-start | bytes 2654208 | tf_op jit(solution)/shard_map/all_gather | solution.py:132
  10.0 256.1 %all-gather.19.cloned.1.call-start = ((), (), s32[]{:S(2)}) async-start(), calls=%async_computation.12 | async-start | bytes 3981312 | tf_op jit(solution)/shard_map/all_gather | solution.py:133
  10.6 296.9 %all-gather.21.cloned.1.call-start = ((), (), s32[]{:S(2)}) async-start(), calls=%async_computation.13 | async-start | bytes 1327104 | tf_op jit(solution)/shard_map/all_gather | solution.py:134
  11.2 377.4 %all-gather.23.cloned.1.call-start = ((), (), s32[]{:S(2)}) async-start(), calls=%async_computation.14 | async-start | bytes 5308416 | tf_op jit(solution)/shard_map/all_gather | solution.py:135
  11.9 456.9 %all-gather.25.cloned.1.call-start = ((), (), s32[]{:S(2)}) async-start(), calls=%async_computation.15 | async-start | bytes 5308416 | tf_op jit(solution)/shard_map/all_gather | solution.py:136
  12.7 614.8 %reduce-scatter.19.cloned.1.call-start = ((), (), s32[]{:S(2)}) async-start(), calls=%async_computation.21 | async-start | bytes 1327104 | tf_op jit(solution)/shard_map/reduce_scatter | solution.py:287
  12.9 187.2 %copy-start.72 = (f32[128]{0:T(128)}, f32[128]{0:T(128)S(1)}, u32[]{:S(2)}) copy-start(f32[128]{0:T(128)S(1)} %broadcast_multiply_fusion.11) | copy-start | bytes 1540
  13.1 187.0 %copy-start.81 = (f32[128]{0:T(128)}, f32[128]{0:T(128)S(1)}, u32[]{:S(2)}) copy-start(f32[128]{0:T(128)S(1)} %add_rsqrt_fusion.3) | copy-start | bytes 1540
  13.8 91.6 %copy-start.52 = (f32[1280]{0:T(1024)}, f32[1280]{0:T(1024)S(1)}, u32[]{:S(2)}) copy-start(f32[1280]{0:T(1024)S(1)} %broadcast_multiply_fusion.2) | copy-start | bytes 15364
  38.1 162.1 %copy-start.56 = (f32[768]{0:T(1024)}, f32[768]{0:T(1024)S(1)}, u32[]{:S(2)}) copy-start(f32[768]{0:T(1024)S(1)} %reshape.631) | copy-start | bytes 9220
  38.1 228.1 %copy-start.45 = (f32[768]{0:T(1024)}, f32[768]{0:T(1024)S(1)}, u32[]{:S(2)}) copy-start(f32[768]{0:T(1024)S(1)} %reshape.635) | copy-start | bytes 9220
  60.3 139.9 %copy-start.42 = (f32[768]{0:T(1024)}, f32[768]{0:T(1024)S(1)}, u32[]{:S(2)}) copy-start(f32[768]{0:T(1024)S(1)} %reshape.630) | copy-start | bytes 9220
  129.6 74.6 %copy-start.30 = (bf16[12,64,128]{2,1,0:T(8,128)(2,1)}, bf16[12,64,128]{2,1,0:T(8,128)(2,1)S(1)}, u32[]{:S(2)}) copy-start(bf16[12,64,128]{2,1,0:T(8,128)(2,1)S(1)} %fusion.45) | copy-start | bytes 589828
  483.6 143.9 %reduce-scatter.13.cloned.1.call-start = ((), (), s32[]{:S(2)}) async-start(), calls=%async_computation.18 | async-start | bytes 1327104 | tf_op jit(solution)/shard_map/reduce_scatter | solution.py:278
  493.9 185.4 %reduce-scatter.9.cloned.1.call-start = ((), (), s32[]{:S(2)}) async-start(), calls=%async_computation.16 | async-start | bytes 1327104 | tf_op jit(solution)/shard_map/reduce_scatter | solution.py:272
  526.0 225.3 %reduce-scatter.15.cloned.1.call-start = ((), (), s32[]{:S(2)}) async-start(), calls=%async_computation.19 | async-start | bytes 2654208 | tf_op jit(solution)/shard_map/reduce_scatter | solution.py:281
  530.3 292.5 %reduce-scatter.11.cloned.1.call-start = ((), (), s32[]{:S(2)}) async-start(), calls=%async_computation.17 | async-start | bytes 2654208 | tf_op jit(solution)/shard_map/reduce_scatter | solution.py:275
  553.3 352.0 %reduce-scatter.17.cloned.1.call-start = ((), (), s32[]{:S(2)}) async-start(), calls=%async_computation.20 | async-start | bytes 3981312 | tf_op jit(solution)/shard_map/reduce_scatter | solution.py:284
  558.1 445.7 %reduce-scatter.23.cloned.1.call-start = ((), (), s32[]{:S(2)}) async-start(), calls=%async_computation.23 | async-start | bytes 5308416 | tf_op jit(solution)/shard_map/reduce_scatter | solution.py:293
  564.2 538.1 %reduce-scatter.21.cloned.1.call-start = ((), (), s32[]{:S(2)}) async-start(), calls=%async_computation.22 | async-start | bytes 5308416 | tf_op jit(solution)/shard_map/reduce_scatter | solution.py:290
  569.8 596.6 %all-reduce.7.cloned.1.call-start = ((), (), s32[]{:S(2)}) async-start(), calls=%async_computation.24 | async-start | bytes 5308416 | tf_op jit(solution)/shard_map/psum | solution.py:304
  (89 other events, 859.9 us)
Sparse Core Ops, SparseCore 0:
  10.3 41.9 all-gather.14
  54.5 50.8 all-gather.12
  107.6 39.5 all-gather.16
  149.2 50.8 all-gather.10
  202.2 63.9 all-gather.18
  268.2 39.2 all-gather.20
  309.7 78.9 all-gather.22
  390.8 78.0 all-gather.24
  483.7 61.5 reduce-scatter.18
  549.1 63.2 reduce-scatter.12
  616.4 62.8 reduce-scatter.8
  682.6 68.5 reduce-scatter.14
  754.7 68.0 reduce-scatter.10
  826.3 78.9 reduce-scatter.16
  908.7 95.0 reduce-scatter.22
  1007.3 95.0 reduce-scatter.20
  1105.0 61.3 all-reduce.6
where the time goes:
time: 1190 us; the launch traced here: 1180 us
  waiting for transfers between devices  899 us (76%)
  matrix products  118 us (10%)
  blocking collectives  86 us (7%)
  local copies, waits for them, and re-layouts  27.3 us (2%)
  other arithmetic  24.5 us (2%)
  between operations  16.3 us (1%)
  starting transfers between devices  13.1 us (1%)
    reduce_scatter x1, waiting for transfers between devices, local(): lax.psum_scatter(gradients[6].astype(jnp.bfloat16), 'fsdp', scatter_dimen...  98.6 us
    reduce_scatter x1, waiting for transfers between devices, local(): lax.psum_scatter(gradients[7].astype(jnp.bfloat16), 'fsdp', scatter_dimen...  98.6 us
    reduce_scatter x1, waiting for transfers between devices, local(): lax.psum_scatter(gradients[4].astype(jnp.bfloat16), 'fsdp', scatter_dimen...  82.5 us
    all_gather x1, waiting for transfers between devices, local(): lax.all_gather(shards[6], 'fsdp', axis=0, tiled=True)  78.2 us
    all_gather x1, waiting for transfers between devices, local(): lax.all_gather(shards[7], 'fsdp', axis=0, tiled=True)  75.9 us
    reduce_scatter x1, waiting for transfers between devices, local(): lax.psum_scatter(gradients[3].astype(jnp.bfloat16), 'fsdp', scatter_dimen...  72 us
    reduce_scatter x1, waiting for transfers between devices, local(): lax.psum_scatter(gradients[1].astype(jnp.bfloat16), 'fsdp', scatter_dimen...  71.5 us
    all_gather x1, waiting for transfers between devices, local(): lax.all_gather(shards[4], 'fsdp', axis=0, tiled=True)  61.7 us
  transfers between devices with their start and end apart: 17, of which 14 were waited for; matrix products, arithmetic and copies ran while one was open for 11% of the time, Pallas kernels for 0%

commit v1 on v0

v1 whole, which is shorter than its diff:
```python
import jax
import jax.numpy as jnp
from jax import lax
from jax.sharding import PartitionSpec as P

H = 12
HD = 64
D = H * HD
BF = jnp.bfloat16
F32 = jnp.float32

epsilon = 1e-05
filtered_logits = -1000000000.0
shared_sheet_reward = 6.0


class Links:
    def __init__(self, reps, shards):
        self.reps, self.shards = reps, shards
        self.depth = shards // 2
        rank = lax.axis_index("rep")
        shard = lax.axis_index("fsdp")
        self.c, self.t = rank % 2, (rank // 2) % 2
        self.group = self.t * 2 + self.c
        self.x, self.z = shard % 2, shard // 2
        self.shard = shard

    def core(self, a):
        return lax.ppermute(a, "rep", [(r, r ^ 1) for r in range(self.reps)])

    def y(self, a):
        return lax.ppermute(a, "rep", [(r, r ^ 2) for r in range(self.reps)])

    def rep_bit(self, a, bit):
        return lax.ppermute(a, "rep", [(r, r ^ bit) for r in range(self.reps)])

    def across(self, a):
        return lax.ppermute(a, "fsdp", [(s, s ^ 1) for s in range(self.shards)])

    def along(self, a, k):
        return lax.ppermute(a, "fsdp", [(s, s ^ (2 * k)) for s in range(self.shards)])

    def gather(self, part, axis=0):
        pieces = [part] + [self.along(part, k) for k in range(1, self.depth)]
        shape = part.shape[:axis] + (self.depth,) + part.shape[axis:]
        column = jnp.zeros(shape, part.dtype)
        for k, piece in enumerate(pieces):
            column = lax.dynamic_update_index_in_dim(column, piece, self.z ^ k, axis)
        other = self.across(column)
        first = self.x == 0
        both = jnp.stack([jnp.where(first, column, other), jnp.where(first, other, column)], axis + 1)
        return both.reshape(part.shape[:axis] + (self.shards,) + part.shape[axis:])

    def scatter(self, whole, axis=0):
        shape = whole.shape
        split = whole.reshape(shape[:axis] + (self.depth, 2) + shape[axis + 1 :])
        keep = lax.dynamic_index_in_dim(split, self.x, axis + 1, False)
        send = lax.dynamic_index_in_dim(split, 1 - self.x, axis + 1, False)
        column = (keep.astype(F32) + self.across(send).astype(F32)).astype(BF)
        total = lax.dynamic_index_in_dim(column, self.z, axis, False).astype(F32)
        for k in range(1, self.depth):
            piece = lax.dynamic_index_in_dim(column, self.z ^ k, axis, False)
            total = total + self.along(piece, k).astype(F32)
        for bit in range(2, self.reps.bit_length() - 1):
            total = total + self.rep_bit(total.astype(BF), 1 << bit).astype(F32)
        return total.astype(BF)

    def spread(self, quarter):
        other_c = self.core(quarter)
        pair = jnp.stack([jnp.where(self.c == 0, quarter, other_c), jnp.where(self.c == 0, other_c, quarter)])
        other_t = self.y(pair)
        return jnp.concatenate([jnp.where(self.t == 0, pair, other_t), jnp.where(self.t == 0, other_t, pair)])

    def total(self, a):
        for bit in range(self.reps.bit_length() - 1):
            a = a + self.rep_bit(a, 1 << bit)
        a = a + self.across(a)
        for bit in range(self.depth.bit_length() - 1):
            a = a + self.along(a, 1 << bit)
        return a

    def place(self, own, oth_c, oth_t, oth_b):
        c0 = self.c == 0
        t0 = self.t == 0
        a, b = jnp.where(c0, own, oth_c), jnp.where(c0, oth_c, own)
        e, f = jnp.where(c0, oth_t, oth_b), jnp.where(c0, oth_b, oth_t)
        return [jnp.where(t0, a, e), jnp.where(t0, b, f), jnp.where(t0, e, a), jnp.where(t0, f, b)]

    def pick(self, a, axis):
        return [lax.dynamic_index_in_dim(a, self.group ^ k, axis, False) for k in range(4)]


def norm_stats(rows):
    mean = jnp.mean(rows, -1, keepdims=True)
    centred = rows - mean
    factor = lax.rsqrt(jnp.mean(centred * centred, -1, keepdims=True) + epsilon)
    return centred * factor, factor


def norm_back(gradient, normal, factor, gain_row):
    scaled = gradient * gain_row
    centred = scaled - jnp.mean(scaled, -1, keepdims=True) - normal * jnp.mean(scaled * normal, -1, keepdims=True)
    return centred * factor, jnp.sum(gradient * normal, 0), jnp.sum(gradient, 0)


def mm(a, b):
    return jnp.dot(a, b, preferred_element_type=F32)


def mm_nt(a, b):
    return lax.dot_general(a, b, (((1,), (1,)), ((), ())), preferred_element_type=F32)


def mm_tn(a, b):
    return lax.dot_general(a, b, (((0,), (0,)), ((), ())), preferred_element_type=F32)


def attend(q, k, v, bias):
    n, m, h = q.shape[0], k.shape[0], q.shape[1] // HD
    q, k, v = q.reshape(n, h, HD), k.reshape(m, h, HD), v.reshape(m, h, HD)
    scores = jnp.einsum("qhe,khe->hqk", q, k, preferred_element_type=F32) * HD ** (-0.5) + bias[None]
    peak = jnp.max(scores, -1, keepdims=True)
    expo = jnp.exp(scores - peak)
    total = jnp.sum(expo, -1, keepdims=True)
    weight = (expo / total).astype(BF)
    out = jnp.einsum("hqk,khe->qhe", weight, v, preferred_element_type=F32)
    return out.reshape(n, h * HD).astype(BF), peak + jnp.log(total)


def attend_back(do, q, k, v, bias, logs):
    n, m, h = q.shape[0], k.shape[0], q.shape[1] // HD
    q, k, v, do = q.reshape(n, h, HD), k.reshape(m, h, HD), v.reshape(m, h, HD), do.reshape(n, h, HD)
    scale = HD ** (-0.5)
    scores = jnp.einsum("qhe,khe->hqk", q, k, preferred_element_type=F32) * scale + bias[None]
    weight = jnp.exp(scores - logs)
    dv = jnp.einsum("hqk,qhe->khe", weight.astype(BF), do, preferred_element_type=F32)
    dp = jnp.einsum("qhe,khe->hqk", do, v, preferred_element_type=F32)
    ds = (weight * (dp - jnp.sum(weight * dp, -1, keepdims=True))).astype(BF)
    dq = jnp.einsum("hqk,khe->qhe", ds, k, preferred_element_type=F32) * scale
    dk = jnp.einsum("hqk,qhe->khe", ds, q, preferred_element_type=F32) * scale
    return dq.reshape(n, h * HD), dk.reshape(m, h * HD), dv.reshape(m, h * HD)


def local(reps, shards, visual, text, visual_valid, block_owner, cross_query, cross_keyval, cross_output, gate_weight,
          self_qkv, self_output, ffn_up, ffn_down, norm_gains, norm_biases, cotangent):
    ln = Links(reps, shards)
    visual, text, cotangent = visual[0], text[0], cotangent[0]
    visual_valid, block_owner = visual_valid[0], block_owner[0]
    rows = cross_query.shape[0]
    quarter = rows // 4
    own = ln.group

    w3 = D // 4
    at = own * w3
    ckv = lax.dynamic_slice_in_dim(cross_keyval.reshape(rows, 2, D), at, w3, 2).reshape(rows, 2 * w3)
    cq = lax.dynamic_slice_in_dim(cross_query, at, w3, 1)
    gains_hi = norm_gains.astype(BF)
    biases_hi = norm_biases.astype(BF)
    gains_lo = (norm_gains - gains_hi.astype(F32)).astype(BF)
    biases_lo = (norm_biases - biases_hi.astype(F32)).astype(BF)
    norms = jnp.concatenate([gains_hi, gains_lo, biases_hi, biases_lo])
    norms = jnp.pad(norms, (0, rows * 64 - norms.shape[0])).reshape(rows, 64)
    part_a = jnp.concatenate([ckv, cq, norms], 1)
    part_b = jnp.concatenate([
        lax.dynamic_slice_in_dim(cross_output, own * quarter, quarter, 0),
        lax.dynamic_slice_in_dim(gate_weight, own * 2 * quarter, 2 * quarter, 0),
        lax.dynamic_slice_in_dim(self_output, own * quarter, quarter, 0)], 0)
    part_c = lax.dynamic_index_in_dim(self_qkv.reshape(rows, 3, 4, w3), own, 2, False).reshape(rows, 3 * w3)
    part_d = jnp.stack([
        lax.dynamic_index_in_dim(ffn_up.reshape(rows, shards, 4, rows), own, 2, False).reshape(rows, D),
        lax.dynamic_index_in_dim(ffn_down.reshape(4, rows, D), own, 0, False)], 0)

    def all_groups(mine):
        mine_t = ln.y(mine)
        pair = ln.core(jnp.stack([mine, mine_t]))
        return mine, pair[0], mine_t, pair[1]

    full_a = all_groups(ln.gather(part_a).reshape(D, -1))
    full_b = all_groups(ln.gather(part_b))
    full_c = ln.gather(part_c).reshape(D, -1)
    full_c = jnp.stack([full_c, ln.core(full_c)])
    full_d = ln.gather(part_d, 1).reshape(2, D, D)
    full_d = (full_d, ln.core(full_d))

    norm_all = full_a[0][:, 3 * w3 :].reshape(shards, rows * 64)
    size = norm_gains.shape[0]
    norm_all = norm_all[:, : 4 * size].astype(F32).reshape(shards, 4, size)
    gain_rows = (norm_all[:, 0] + norm_all[:, 1]).reshape(4, D)
    biases = (norm_all[:, 2] + norm_all[:, 3]).reshape(4, D)
    kv_w = [w[:, : 2 * w3] for w in full_a]
    q_w = [w[:, 2 * w3 : 3 * w3] for w in full_a]
    placed = jnp.stack(ln.place(*full_b), 1)
    out_w = placed[:, :, :quarter].reshape(D, D)
    gate_w = placed[:, :, quarter : 3 * quarter].reshape(2 * D, D)
    self_out_w = placed[:, :, 3 * quarter :].reshape(D, D)

    def pair_y(a):
        return jnp.stack([a, ln.y(a)])

    cot_pair = pair_y(cotangent)
    bias_pair = pair_y(jnp.where(visual_valid > 0, 0.0, filtered_logits).astype(F32))
    visual_rows = visual.astype(F32)
    normal_one, factor_one = norm_stats(visual_rows)
    normed = (normal_one * gain_rows[0] + biases[0]).astype(BF)
    normal_text, factor_text = norm_stats(text.astype(F32))
    text_normed = (normal_text * gain_rows[1] + biases[1]).astype(BF)
    queries = jnp.concatenate([mm(normed, w) for w in q_w], 1).astype(BF)
    keyvals = [mm(text_normed, w).astype(BF) for w in kv_w]
    keys = jnp.concatenate([a[:, :w3] for a in keyvals], 1)
    values = jnp.concatenate([a[:, w3:] for a in keyvals], 1)
    vis = visual.shape[0]
    parent = block_owner[None, :] == lax.broadcasted_iota(jnp.int32, (vis, 1), 0)
    present = jnp.sum(jnp.where(parent, visual_valid[:, None], 0), axis=0) > 0
    cross_bias = jnp.where(parent, shared_sheet_reward, 0.0) + jnp.where(present, 0.0, filtered_logits)[None, :]
    mixed_rel, cross_log = attend(queries, keys, values, cross_bias)
    mixed = jnp.concatenate(ln.place(*jnp.split(mixed_rel, 4, 1)), 1)
    cross_rows = mm(mixed, out_w).astype(BF)
    cross_full = cross_rows.astype(F32)
    gate = jax.nn.sigmoid(mm(jnp.concatenate([normed, cross_rows], 1), gate_w))
    joined = visual_rows + gate * cross_full
    normal_two, factor_two = norm_stats(joined)
    second = (normal_two * gain_rows[2] + biases[2]).astype(BF)
    second2 = pair_y(second).reshape(2 * vis, D)
    triple = [mm(second2, full_c[i]).astype(BF).reshape(2, vis, 3, w3) for i in range(2)]
    triple = jnp.stack(triple, 3).reshape(2, vis, 3, 2 * w3)
    self_bias = jnp.broadcast_to(bias_pair[:, None, :], (2, vis, vis))
    self_fwd = [attend(triple[p, :, 0], triple[p, :, 1], triple[p, :, 2], self_bias[p]) for p in range(2)]
    att_mine = self_fwd[0][0]
    att_from = ln.y(self_fwd[1][0])
    attended = jnp.concatenate(ln.place(att_mine[:, :w3], att_mine[:, w3:], att_from[:, :w3], att_from[:, w3:]), 1)
    carried = joined + mm(attended, self_out_w)
    normal_three, factor_three = norm_stats(carried)
    third = (normal_three * gain_rows[3] + biases[3]).astype(BF)
    third2 = pair_y(third).reshape(2 * vis, D)
    lifted = [mm(third2, w[0]) for w in full_d]
    acts = [jax.vjp(lambda v: jax.nn.gelu(v, approximate=True), l) for l in lifted]
    active = [a[0].astype(BF) for a in acts]
    down = (mm(active[0], full_d[0][1]) + mm(active[1], full_d[1][1])).reshape(2, vis, D)
    layer_out = (carried + down[0] + ln.y(down[1].astype(BF)).astype(F32)).astype(BF)

    cot2 = cot_pair.reshape(2 * vis, D)
    d_down = [mm_tn(a, cot2).astype(BF) for a in active]
    d_lifted = [acts[i][1](mm_nt(cot2, full_d[i][1]))[0].astype(BF) for i in range(2)]
    d_up = [mm_tn(third2, d).astype(BF) for d in d_lifted]

    def scatter_core(mine, other, axis):
        both = (mine.astype(F32) + ln.core(other).astype(F32)).astype(BF)
        return ln.scatter(both.reshape(both.shape[:axis] + (shards, rows) + both.shape[axis + 1 :]), axis)

    sum_d = scatter_core(jnp.stack([d_up[0], d_down[0]]), jnp.stack([d_up[1], d_down[1]]), 1)
    d_third = (mm_nt(d_lifted[0], full_d[0][0]) + mm_nt(d_lifted[1], full_d[1][0])).reshape(2, vis, D)
    d_third = d_third[0] + ln.y(d_third[1].astype(BF)).astype(F32)
    back_three, gain_three, bias_three = norm_back(d_third, normal_three, factor_three, gain_rows[3])
    d_carried = cotangent.astype(F32) + back_three
    carried_low = d_carried.astype(BF)
    d_self_output = mm_tn(attended, carried_low).astype(BF)
    d_attended = mm_nt(carried_low, self_out_w).astype(BF)
    d_att = ln.pick(d_attended.reshape(vis, 4, w3), 1)
    from_y = ln.y(jnp.concatenate([d_att[2], d_att[3]], 1))
    d_att = [jnp.concatenate([d_att[0], d_att[1]], 1), from_y]
    self_back = [attend_back(d_att[p], triple[p, :, 0], triple[p, :, 1], triple[p, :, 2], self_bias[p], self_fwd[p][1])
                 for p in range(2)]
    d_triple = jnp.stack([jnp.stack([g.reshape(vis, 2, w3) for g in page], 2) for page in self_back])
    d_triple = d_triple.astype(BF).reshape(2 * vis, 2, 3 * w3)
    d_triple = [d_triple[:, 0], d_triple[:, 1]]
    d_qkv = [mm_tn(second2, g).astype(BF) for g in d_triple]
    sum_c = scatter_core(d_qkv[0], d_qkv[1], 0)
    d_second = (mm_nt(d_triple[0], full_c[0]) + mm_nt(d_triple[1], full_c[1])).reshape(2, vis, D)
    d_second = d_second[0] + ln.y(d_second[1].astype(BF)).astype(F32)
    back_two, gain_two, bias_two = norm_back(d_second, normal_two, factor_two, gain_rows[2])
    d_joined = d_carried + back_two
    d_gate_in = (d_joined * cross_full * gate * (1.0 - gate)).astype(BF)
    d_gate_w = jnp.concatenate([mm_tn(normed, d_gate_in), mm_tn(cross_rows, d_gate_in)], 0).astype(BF)
    d_gate_rows = mm_nt(d_gate_in, gate_w)
    d_cross = (d_joined * gate + d_gate_rows[:, D:]).astype(BF)
    d_out_w = mm_tn(mixed, d_cross).astype(BF)
    stacked_b = jnp.concatenate([
        d_out_w.reshape(shards, 4, quarter, D),
        d_gate_w.reshape(shards, 4, 2 * quarter, D),
        d_self_output.reshape(shards, 4, quarter, D)], 2)

    def scatter_groups(groups):
        got = ln.core(jnp.stack([groups[1], groups[3]]))
        first = (groups[0].astype(F32) + got[0].astype(F32)).astype(BF)
        second_ = (groups[2].astype(F32) + got[1].astype(F32)).astype(BF)
        return ln.scatter((first.astype(F32) + ln.y(second_).astype(F32)).astype(BF))

    sum_b = scatter_groups(ln.pick(stacked_b, 1))
    d_mixed = mm_nt(d_cross, out_w).astype(BF)
    d_mixed = jnp.concatenate(ln.pick(d_mixed.reshape(vis, 4, w3), 1), 1)
    d_q, d_k, d_v = attend_back(d_mixed, queries, keys, values, cross_bias, cross_log)
    d_q = jnp.split(d_q.astype(BF), 4, 1)
    d_kv = [jnp.concatenate([k_, v_], 1).astype(BF) for k_, v_ in zip(jnp.split(d_k, 4, 1), jnp.split(d_v, 4, 1))]
    groups_a = [jnp.concatenate([mm_tn(text_normed, d_kv[g]), mm_tn(normed, d_q[g])], 1).astype(BF).reshape(shards, rows, 3 * w3)
                for g in range(4)]
    sum_a = scatter_groups(groups_a)
    d_normed = mm_nt(d_gate_in, gate_w[:D])
    d_text_normed = 0.0
    for g in range(4):
        d_normed = d_normed + mm_nt(d_q[g], q_w[g])
        d_text_normed = d_text_normed + mm_nt(d_kv[g], kv_w[g])
    back_one, gain_one, bias_one = norm_back(d_normed, normal_one, factor_one, gain_rows[0])
    grad_visual = d_joined + back_one
    grad_text, gain_text, bias_text = norm_back(d_text_normed, normal_text, factor_text, gain_rows[1])
    norm_grads = jnp.stack([gain_one, gain_text, gain_two, gain_three, bias_one, bias_text, bias_two, bias_three])
    norm_grads = ln.total(norm_grads).reshape(2, shards, size)
    norm_grads = lax.dynamic_index_in_dim(norm_grads, ln.shard, 1, False)

    all_a = ln.spread(sum_a).astype(F32)
    all_b = ln.spread(sum_b).astype(F32)
    all_c = ln.spread(sum_c).astype(F32)
    all_d = ln.spread(sum_d).astype(F32)
    g_keyval = all_a[:, :, : 2 * w3].reshape(4, rows, 2, w3).transpose(1, 2, 0, 3).reshape(rows, 2 * D)
    g_query = all_a[:, :, 2 * w3 :].transpose(1, 0, 2).reshape(rows, D)
    g_out = all_b[:, :quarter].reshape(rows, D)
    g_gate = all_b[:, quarter : 3 * quarter].reshape(2 * rows, D)
    g_self_out = all_b[:, 3 * quarter :].reshape(rows, D)
    g_qkv = all_c.reshape(4, rows, 3, w3).transpose(1, 2, 0, 3).reshape(rows, 3 * D)
    g_up = all_d[:, 0].reshape(4, rows, shards, rows).transpose(1, 2, 0, 3).reshape(rows, 4 * D)
    g_down = all_d[:, 1].reshape(4 * rows, D)
    return (layer_out[None], grad_visual[None], grad_text[None], g_query, g_keyval, g_out, g_gate, g_qkv, g_self_out,
            g_up, g_down, norm_grads[0], norm_grads[1])


def solution(mesh):
    pages = P(("rep", "fsdp"), None, None)
    flags = P(("rep", "fsdp"), None)
    matrix = P("fsdp", None)
    vector = P("fsdp")
    in_specs = (pages, pages, flags, flags) + (matrix,) * 8 + (vector, vector, pages)
    out_specs = (pages, pages, pages) + (matrix,) * 8 + (vector, vector)
    reps, shards = mesh.shape["rep"], mesh.shape["fsdp"]

    def run(*args):
        return local(reps, shards, *args)

    return jax.shard_map(run, mesh=mesh, in_specs=in_specs, out_specs=out_specs, check_vma=False)
```

time: 1190 us -> 559 us (0.47)
  waiting for transfers between devices: 899 us -> 104 us
  local copies, waits for them, and re-layouts: 27.3 us -> 134 us
  starting transfers between devices: 13.1 us -> 112 us
  blocking collectives: 86 us -> 0 us
  other arithmetic: 24.5 us -> 82.1 us
  between operations: 16.3 us -> 3.75 us
    reduce_scatter x8 -> x0, waiting for transfers between devices: 475 us -> none  [the longest x1 98.6 us: local(): lax.psum_scatter(gradients[6].astype(jnp.bfloat16), 'fsdp', scatter_dimen...]
    all_gather x8 -> x0, waiting for transfers between devices: 362 us -> none  [the longest x1 78.2 us: local(): lax.all_gather(shards[6], 'fsdp', axis=0, tiled=True)]
    ppermute x0 -> x66, starting transfers between devices: none -> 112 us  [the longest x12 48.7 us: core(): return lax.ppermute(a, 'rep', [(r, r ^ 1) for r in range(self.reps)])]
    ppermute x0 -> x66, waiting for transfers between devices: none -> 104 us  [the longest x26 57 us: along(): return lax.ppermute(a, 'fsdp', [(s, s ^ 2 * k) for s in range(self.shards)])]
    psum x1 -> x0, waiting for transfers between devices: 56.6 us -> none  [local(): lax.psum(shares[0].astype(jnp.bfloat16), 'rep').astype(jnp.float32)]
    all_gather x2 -> x0, blocking collectives: 44.9 us -> none  [the longest x1 22.9 us: local(): lax.all_gather(shards[9].astype(jnp.bfloat16), 'fsdp', axis=0, tiled=True)]
    another operation x1 -> x34, other arithmetic: 0.29 us -> 29 us  [the longest x9 8.94 us: gather(): jnp.stack([jnp.where(first, column, other), jnp.where(first, other, colum...]
    unnamed x1 -> x0, blocking collectives: 28.2 us -> none
  transfers between devices with their start and end apart: 17 -> 66, of which waited for: 14 -> 27; matrix products, arithmetic and copies ran while one was open for 11% -> 57% of each run, Pallas kernels for 0% -> 0%
where the time goes in v1:
time: 559 us; the launch traced here: 552 us
  local copies, waits for them, and re-layouts  134 us (24%)
  matrix products  116 us (21%)
  starting transfers between devices  112 us (20%)
  waiting for transfers between devices  104 us (19%)
  other arithmetic  82.1 us (15%)
    ppermute x26, waiting for transfers between devices, along(): return lax.ppermute(a, 'fsdp', [(s, s ^ 2 * k) for s in range(self.shards)])  57 us
    ppermute x12, starting transfers between devices, core(): return lax.ppermute(a, 'rep', [(r, r ^ 1) for r in range(self.reps)])  48.7 us
    dot_general x18, matrix products, mm_nt(): lax.dot_general(a, b, (((1,), (1,)), ((), ())), preferred_element_type=F32)  36 us
    ppermute x26, starting transfers between devices, along(): return lax.ppermute(a, 'fsdp', [(s, s ^ 2 * k) for s in range(self.shards)])  31.3 us
    ppermute x17, waiting for transfers between devices, y(): return lax.ppermute(a, 'rep', [(r, r ^ 2) for r in range(self.reps)])  28.5 us
    dot_general x18, matrix products, mm_tn(): lax.dot_general(a, b, (((0,), (0,)), ((), ())), preferred_element_type=F32)  28 us
    dot_general x17, matrix products, mm(): return jnp.dot(a, b, preferred_element_type=F32)  27.9 us
    unnamed x325, local copies, waits for them, and re-layouts  24.5 us
  transfers between devices with their start and end apart: 66, of which 27 were waited for; matrix products, arithmetic and copies ran while one was open for 57% of the time, Pallas kernels for 0%

profile of v1, /device:TPU:1, one launch (start us, length us, event | category | flops | bytes accessed | tf_op | source)
XLA Modules:
  0.0 551.7 jit_solution(3413221346009157863)
XLA Ops:
  36.2 3.7 collective-permute-done.15
  47.8 6.4 %collective-permute-start.21 = (bf16[2,96,768]{2,1,0:T(8,128)(2,1)}, bf16[2,96,768]{2,1,0:T(8,128)(2,1)S(1)}, u32[]{:S(2)}, u32[]{:S(2)}) collective-permute-start(bf16[2,96,768]{2,1,0:T(8,128)(2,1)} %pad_maximum_fusion.32), channel_id=1, source_target_pairs={{0,2},{1,3},{2,0},{3,1},{4,6},{5,7},{6,4},{7,5},{8,10},{9,11},{10,... | collective-permute-start | bytes 884744 | tf_op jit(solution)/shard_map/ppermute | solution.py:41
  73.6 21.0 %collective-permute-start.17 = (bf16[768,576]{0,1:T(8,128)(2,1)}, bf16[768,576]{0,1:T(8,128)(2,1)}, u32[]{:S(2)}, u32[]{:S(2)}) collective-permute-start(bf16[768,576]{0,1:T(8,128)(2,1)} %copy.208), channel_id=1, source_target_pairs={{0,8},{8,0},{16,24},{24,16},{1,9},{9,1},{17,25},{25,17},{2,10},{10... | collective-permute-start | bytes 2654216 | tf_op jit(solution)/shard_map/ppermute | solution.py:29
  114.3 3.6 convolution_convert_fusion.3
  121.4 4.1 copy.244
  134.6 9.7 %collective-permute-start.5 = (bf16[2,768,640]{2,1,0:T(8,128)(2,1)}, bf16[2,768,640]{2,1,0:T(8,128)(2,1)}, u32[]{:S(2)}, u32[]{:S(2)}) collective-permute-start(bf16[2,768,640]{2,1,0:T(8,128)(2,1)} %pad_maximum_fusion.7), channel_id=1, source_target_pairs={{0,8},{8,0},{16,24},{24,16},{1,9},{9,1},{17,25},{25,17},{2,10},{10... | collective-permute-start | bytes 5898248 | tf_op jit(solution)/shard_map/ppermute | solution.py:29
  195.5 4.7 collective-permute-done.12
  240.3 3.8 collective-permute-start.54
  286.4 4.9 fusion.22
  291.3 4.6 multiply_reduce_fusion
  318.1 4.8 fusion.83
  327.1 4.4 fusion.90
  347.0 4.1 fusion.35
  356.0 5.2 fusion.16
  386.0 5.2 collective-permute-done.63
  400.5 5.2 collective-permute-done.50
  418.3 14.1 %collective-permute-done.32 = bf16[8,96,576]{2,1,0:T(8,128)(2,1)} collective-permute-done((bf16[8,96,576]{2,1,0:T(8,128)(2,1)S(1)}, bf16[8,96,576]{2,1,0:T(8,128)(2,1)}, u32[]{:S(2)}, u32[]{:S(2)}) %collective-permute-start.32) | collective-permute-done | bytes 884768 | tf_op jit(solution)/shard_map/ppermute | solution.py:32
  462.2 7.2 %collective-permute-done.35 = bf16[96,576]{1,0:T(8,128)(2,1)S(1)} collective-permute-done((bf16[96,576]{1,0:T(8,128)(2,1)S(1)}, bf16[96,576]{1,0:T(8,128)(2,1)S(1)}, u32[]{:S(2)}, u32[]{:S(2)}) %collective-permute-start.35) | collective-permute-done | bytes 110624 | tf_op jit(solution)/shard_map/ppermute | solution.py:41
  475.5 4.7 collective-permute-done.56
  480.2 5.7 %collective-permute-done.58 = bf16[2,96,768]{2,1,0:T(8,128)(2,1)S(1)} collective-permute-done((bf16[2,96,768]{2,1,0:T(8,128)(2,1)S(1)}, bf16[2,96,768]{2,1,0:T(8,128)(2,1)S(1)}, u32[]{:S(2)}, u32[]{:S(2)}) %collective-permute-start.58) | collective-permute-done | bytes 294944 | tf_op jit(solution)/shard_map/ppermute | solution.py:41
  485.9 13.8 %collective-permute-done.57 = bf16[2,96,768]{2,1,0:T(8,128)(2,1)S(1)} collective-permute-done((bf16[2,96,768]{2,1,0:T(8,128)(2,1)S(1)}, bf16[2,96,768]{2,1,0:T(8,128)(2,1)S(1)}, u32[]{:S(2)}, u32[]{:S(2)}) %collective-permute-start.57) | collective-permute-done | bytes 294944 | tf_op jit(solution)/shard_map/ppermute | solution.py:41
  511.6 7.7 %collective-permute-done.41 = bf16[4,96,768]{2,1,0:T(8,128)(2,1)} collective-permute-done((bf16[4,96,768]{2,1,0:T(8,128)(2,1)}, bf16[4,96,768]{2,1,0:T(8,128)(2,1)}, u32[]{:S(2)}, u32[]{:S(2)}) %collective-permute-start.41) | collective-permute-done | bytes 589856 | tf_op jit(solution)/shard_map/ppermute | solution.py:38
  528.4 7.5 %collective-permute-done.43 = bf16[96,768]{1,0:T(8,128)(2,1)S(1)} collective-permute-done((bf16[96,768]{1,0:T(8,128)(2,1)S(1)}, bf16[96,768]{1,0:T(8,128)(2,1)S(1)}, u32[]{:S(2)}, u32[]{:S(2)}) %collective-permute-start.43) | collective-permute-done | bytes 147488 | tf_op jit(solution)/shard_map/ppermute | solution.py:41
  545.9 3.6 reshape.649
  (753 shorter events, 388.2 us)
Async XLA Ops:
  3.3 54.2 %collective-permute-start.7 = (bf16[96,768]{1,0:T(8,128)(2,1)}, bf16[96,768]{1,0:T(8,128)(2,1)}, u32[]{:S(2)}, u32[]{:S(2)}) collective-permute-start(bf16[96,768]{1,0:T(8,128)(2,1)} %pad_maximum_fusion.40), channel_id=1, source_target_pairs={{0,4},{1,5},{2,6},{3,7},{4,0},{5,1},{6,2},{7,3},{8,12},{9,13},{10,... | collective-permute-start | bytes 442376 | tf_op jit(solution)/shard_map/ppermute | solution.py:41
  6.4 47.8 %collective-permute-start.6 = (bf16[96,768]{1,0:T(8,128)(2,1)}, bf16[96,768]{1,0:T(8,128)(2,1)}, u32[]{:S(2)}, u32[]{:S(2)}) collective-permute-start(bf16[96,768]{1,0:T(8,128)(2,1)} %pad_maximum_fusion.40), channel_id=1, source_target_pairs={{0,2},{1,3},{2,0},{3,1},{4,6},{5,7},{6,4},{7,5},{8,10},{9,11},{10,... | collective-permute-start | bytes 442376 | tf_op jit(solution)/shard_map/ppermute | solution.py:41
  7.7 51.6 %collective-permute-start.8 = (bf16[96,768]{1,0:T(8,128)(2,1)}, bf16[96,768]{1,0:T(8,128)(2,1)}, u32[]{:S(2)}, u32[]{:S(2)}) collective-permute-start(bf16[96,768]{1,0:T(8,128)(2,1)} %pad_maximum_fusion.40), channel_id=1, source_target_pairs={{0,6},{1,7},{2,4},{3,5},{4,2},{5,3},{6,0},{7,1},{8,14},{9,15},{10,... | collective-permute-start | bytes 442376 | tf_op jit(solution)/shard_map/ppermute | solution.py:41
  45.6 21.5 %collective-permute-start.22 = (bf16[2,96,768]{2,1,0:T(8,128)(2,1)}, bf16[2,96,768]{2,1,0:T(8,128)(2,1)S(1)}, u32[]{:S(2)}, u32[]{:S(2)}) collective-permute-start(bf16[2,96,768]{2,1,0:T(8,128)(2,1)} %pad_maximum_fusion.32), channel_id=1, source_target_pairs={{0,4},{1,5},{2,6},{3,7},{4,0},{5,1},{6,2},{7,3},{8,12},{9,13},{10,... | collective-permute-start | bytes 884744 | tf_op jit(solution)/shard_map/ppermute | solution.py:41
  57.5 154.8 %collective-permute-start.18 = (f32[128]{0:T(128)}, f32[128]{0:T(128)}, u32[]{:S(2)}, u32[]{:S(2)}) collective-permute-start(f32[128]{0:T(128)} %compare_select_fusion.1), channel_id=1, source_target_pairs={{0,16},{8,24},{16,0},{24,8},{1,17},{9,25},{17,1},{25,9},{2,18},{10... | collective-permute-start | bytes 1544 | tf_op jit(solution)/shard_map/ppermute | solution.py:32
  66.1 28.5 %collective-permute-start.3 = (bf16[4,96,640]{2,1,0:T(8,128)(2,1)S(1)}, bf16[4,96,640]{2,1,0:T(8,128)(2,1)}, u32[]{:S(2)}, u32[]{:S(2)}) collective-permute-start(bf16[4,96,640]{2,1,0:T(8,128)(2,1)S(1)} %bitcast_dynamic-update-slice_fusion.8), channel_id=1, source_target_pairs={{0,1},{1,0},{2,3},{3,2},{4,5},{5,4},{6,7},{7,6},{8,9},{9,8},{10,11... | collective-permute-start | bytes 1474568 | tf_op jit(solution)/shard_map/ppermute | solution.py:38
  67.1 60.6 %collective-permute-start.9 = (bf16[4,96,768]{2,1,0:T(8,128)(2,1)}, bf16[4,96,768]{2,1,0:T(8,128)(2,1)}, u32[]{:S(2)}, u32[]{:S(2)}) collective-permute-start(bf16[4,96,768]{2,1,0:T(8,128)(2,1)} %bitcast_dynamic-update-slice_fusion.4), channel_id=1, source_target_pairs={{0,1},{1,0},{2,3},{3,2},{4,5},{5,4},{6,7},{7,6},{8,9},{9,8},{10,11... | collective-permute-start | bytes 1769480 | tf_op jit(solution)/shard_map/ppermute | solution.py:38
  69.8 74.5 %collective-permute-start.24 = (bf16[2,4,96,768]{3,2,1,0:T(8,128)(2,1)}, bf16[2,4,96,768]{3,2,1,0:T(8,128)(2,1)}, u32[]{:S(2)}, u32[]{:S(2)}) collective-permute-start(bf16[2,4,96,768]{3,2,1,0:T(8,128)(2,1)} %bitcast_dynamic-update-slice_fusion), channel_id=1, source_target_pairs={{0,1},{1,0},{2,3},{3,2},{4,5},{5,4},{6,7},{7,6},{8,9},{9,8},{10,11... | collective-permute-start | bytes 3538952 | tf_op jit(solution)/shard_map/ppermute | solution.py:38
  73.6 127.9 %collective-permute-start.17 = (bf16[768,576]{0,1:T(8,128)(2,1)}, bf16[768,576]{0,1:T(8,128)(2,1)}, u32[]{:S(2)}, u32[]{:S(2)}) collective-permute-start(bf16[768,576]{0,1:T(8,128)(2,1)} %copy.208), channel_id=1, source_target_pairs={{0,8},{8,0},{16,24},{24,16},{1,9},{9,1},{17,25},{25,17},{2,10},{10... | collective-permute-start | bytes 2654216 | tf_op jit(solution)/shard_map/ppermute | solution.py:29
  99.0 32.6 %collective-permute-start.4 = (bf16[768,640]{1,0:T(8,128)(2,1)}, bf16[768,640]{1,0:T(8,128)(2,1)}, u32[]{:S(2)}, u32[]{:S(2)}) collective-permute-start(bf16[768,640]{1,0:T(8,128)(2,1)} %bitcast.7), channel_id=1, source_target_pairs={{0,16},{8,24},{16,0},{24,8},{1,17},{9,25},{17,1},{25,9},{2,18},{10... | collective-permute-start | bytes 2949128 | tf_op jit(solution)/shard_map/ppermute | solution.py:32
  130.2 26.7 %collective-permute-start.10 = (bf16[8,96,768]{2,1,0:T(8,128)(2,1)}, bf16[8,96,768]{2,1,0:T(8,128)(2,1)}, u32[]{:S(2)}, u32[]{:S(2)}) collective-permute-start(bf16[8,96,768]{2,1,0:T(8,128)(2,1)} %bitcast.38), channel_id=1, source_target_pairs={{0,16},{8,24},{16,0},{24,8},{1,17},{9,25},{17,1},{25,9},{2,18},{10... | collective-permute-start | bytes 3538952 | tf_op jit(solution)/shard_map/ppermute | solution.py:32
  134.6 27.5 %collective-permute-start.5 = (bf16[2,768,640]{2,1,0:T(8,128)(2,1)}, bf16[2,768,640]{2,1,0:T(8,128)(2,1)}, u32[]{:S(2)}, u32[]{:S(2)}) collective-permute-start(bf16[2,768,640]{2,1,0:T(8,128)(2,1)} %pad_maximum_fusion.7), channel_id=1, source_target_pairs={{0,8},{8,0},{16,24},{24,16},{1,9},{9,1},{17,25},{25,17},{2,10},{10... | collective-permute-start | bytes 5898248 | tf_op jit(solution)/shard_map/ppermute | solution.py:29
  147.7 80.6 %collective-permute-start.25 = (bf16[2,768,768]{2,1,0:T(8,128)(2,1)}, bf16[2,768,768]{2,1,0:T(8,128)(2,1)}, u32[]{:S(2)}, u32[]{:S(2)}) collective-permute-start(bf16[2,768,768]{2,1,0:T(8,128)(2,1)} %bitcast.92), channel_id=1, source_target_pairs={{0,8},{8,0},{16,24},{24,16},{1,9},{9,1},{17,25},{25,17},{2,10},{10... | collective-permute-start | bytes 7077896 | tf_op jit(solution)/shard_map/ppermute | solution.py:29
  160.1 24.1 %collective-permute-start.11 = (bf16[2,8,96,768]{3,2,1,0:T(8,128)(2,1)}, bf16[2,8,96,768]{3,2,1,0:T(8,128)(2,1)}, u32[]{:S(2)}, u32[]{:S(2)}) collective-permute-start(bf16[2,8,96,768]{3,2,1,0:T(8,128)(2,1)} %pad_maximum_fusion.3), channel_id=1, source_target_pairs={{0,8},{8,0},{16,24},{24,16},{1,9},{9,1},{17,25},{25,17},{2,10},{10... | collective-permute-start | bytes 7077896 | tf_op jit(solution)/shard_map/ppermute | solution.py:29
  240.3 172.7 %collective-permute-start.54 = (bf16[2,768,768]{2,1,0:T(8,128)(2,1)}, bf16[2,768,768]{2,1,0:T(8,128)(2,1)}, u32[]{:S(2)}, u32[]{:S(2)}) collective-permute-start(bf16[2,768,768]{2,1,0:T(8,128)(2,1)} %pad_maximum_fusion.6), channel_id=1, source_target_pairs={{0,8},{8,0},{16,24},{24,16},{1,9},{9,1},{17,25},{25,17},{2,10},{10... | collective-permute-start | bytes 7077896 | tf_op jit(solution)/shard_map/ppermute | solution.py:29
  275.5 100.1 %collective-permute-start.47 = (bf16[768,576]{0,1:T(8,128)(2,1)}, bf16[768,576]{0,1:T(8,128)(2,1)}, u32[]{:S(2)}, u32[]{:S(2)}) collective-permute-start(bf16[768,576]{0,1:T(8,128)(2,1)} %convolution_convert_fusion.12), channel_id=1, source_target_pairs={{0,8},{8,0},{16,24},{24,16},{1,9},{9,1},{17,25},{25,17},{2,10},{10... | collective-permute-start | bytes 2654216 | tf_op jit(solution)/shard_map/ppermute | solution.py:29
  367.5 40.0 %collective-permute-start.31 = (bf16[2,8,96,576]{3,2,1,0:T(8,128)(2,1)}, bf16[2,8,96,576]{3,2,1,0:T(8,128)(2,1)}, u32[]{:S(2)}, u32[]{:S(2)}) collective-permute-start(bf16[2,8,96,576]{3,2,1,0:T(8,128)(2,1)} %maximum_maximum_fusion), channel_id=1, source_target_pairs={{0,8},{8,0},{16,24},{24,16},{1,9},{9,1},{17,25},{25,17},{2,10},{10... | collective-permute-start | bytes 5308424 | tf_op jit(solution)/shard_map/ppermute | solution.py:29
  395.8 54.3 %collective-permute-start.39 = (bf16[2,8,96,768]{3,2,1,0:T(8,128)(2,1)}, bf16[2,8,96,768]{3,2,1,0:T(8,128)(2,1)}, u32[]{:S(2)}, u32[]{:S(2)}) collective-permute-start(bf16[2,8,96,768]{3,2,1,0:T(8,128)(2,1)} %pad_maximum_fusion.5), channel_id=1, source_target_pairs={{0,8},{8,0},{16,24},{24,16},{1,9},{9,1},{17,25},{25,17},{2,10},{10... | collective-permute-start | bytes 7077896 | tf_op jit(solution)/shard_map/ppermute | solution.py:29
  408.9 23.5 %collective-permute-start.32 = (bf16[8,96,576]{2,1,0:T(8,128)(2,1)S(1)}, bf16[8,96,576]{2,1,0:T(8,128)(2,1)}, u32[]{:S(2)}, u32[]{:S(2)}) collective-permute-start(bf16[8,96,576]{2,1,0:T(8,128)(2,1)S(1)} %fusion.29), channel_id=1, source_target_pairs={{0,16},{8,24},{16,0},{24,8},{1,17},{9,25},{17,1},{25,9},{2,18},{10... | collective-permute-start | bytes 2654216 | tf_op jit(solution)/shard_map/ppermute | solution.py:32
  413.0 24.7 %collective-permute-start.53 = (bf16[2,96,576]{2,1,0:T(8,128)(2,1)S(1)}, bf16[2,96,576]{2,1,0:T(8,128)(2,1)S(1)}, u32[]{:S(2)}, u32[]{:S(2)}) collective-permute-start(bf16[2,96,576]{2,1,0:T(8,128)(2,1)S(1)} %pad_maximum_fusion.35), channel_id=1, source_target_pairs={{0,16},{8,24},{16,0},{24,8},{1,17},{9,25},{17,1},{25,9},{2,18},{10... | collective-permute-start | bytes 663560 | tf_op jit(solution)/shard_map/ppermute | solution.py:32
  417.1 41.7 %collective-permute-start.55 = (bf16[2,4,96,768]{3,2,1,0:T(8,128)(2,1)}, bf16[2,4,96,768]{3,2,1,0:T(8,128)(2,1)}, u32[]{:S(2)}, u32[]{:S(2)}) collective-permute-start(bf16[2,4,96,768]{3,2,1,0:T(8,128)(2,1)} %dynamic-slice_bitcast_fusion), channel_id=1, source_target_pairs={{0,1},{1,0},{2,3},{3,2},{4,5},{5,4},{6,7},{7,6},{8,9},{9,8},{10,11... | collective-permute-start | bytes 3538952 | tf_op jit(solution)/shard_map/ppermute | solution.py:38
  452.0 49.1 %collective-permute-start.40 = (bf16[8,96,768]{2,1,0:T(8,128)(2,1)S(1)}, bf16[8,96,768]{2,1,0:T(8,128)(2,1)S(1)}, u32[]{:S(2)}, u32[]{:S(2)}) collective-permute-start(bf16[8,96,768]{2,1,0:T(8,128)(2,1)S(1)} %fusion.27), channel_id=1, source_target_pairs={{0,16},{8,24},{16,0},{24,8},{1,17},{9,25},{17,1},{25,9},{2,18},{10... | collective-permute-start | bytes 3538952 | tf_op jit(solution)/shard_map/ppermute | solution.py:32
  472.3 27.4 %collective-permute-start.57 = (bf16[2,96,768]{2,1,0:T(8,128)(2,1)S(1)}, bf16[2,96,768]{2,1,0:T(8,128)(2,1)S(1)}, u32[]{:S(2)}, u32[]{:S(2)}) collective-permute-start(bf16[2,96,768]{2,1,0:T(8,128)(2,1)S(1)} %get-tuple-element.69), channel_id=1, source_target_pairs={{0,4},{1,5},{2,6},{3,7},{4,0},{5,1},{6,2},{7,3},{8,12},{9,13},{10,... | collective-permute-start | bytes 884744 | tf_op jit(solution)/shard_map/ppermute | solution.py:41
  474.0 31.2 %collective-permute-start.38 = (bf16[2,96,576]{2,1,0:T(8,128)(2,1)S(1)}, bf16[2,96,576]{2,1,0:T(8,128)(2,1)S(1)}, u32[]{:S(2)}, u32[]{:S(2)}) collective-permute-start(bf16[2,96,576]{2,1,0:T(8,128)(2,1)S(1)} %pad_maximum_fusion.34), channel_id=1, source_target_pairs={{0,16},{8,24},{16,0},{24,8},{1,17},{9,25},{17,1},{25,9},{2,18},{10... | collective-permute-start | bytes 663560 | tf_op jit(solution)/shard_map/ppermute | solution.py:32
  (200 other events, 1174.7 us)

commit v2 on v1

v2 whole, which is shorter than its diff:
```python
import functools

import jax
import jax.numpy as jnp
from jax import lax
from jax.experimental import pallas as pl
from jax.experimental.pallas import tpu as pltpu
from jax.sharding import PartitionSpec as P

H = 12
HD = 64
D = H * HD
HALF = D // 2
QUART = D // 4
BF = jnp.bfloat16
F32 = jnp.float32

epsilon = 1e-05
filtered_logits = -1000000000.0
shared_sheet_reward = 6.0
SCALE = HD ** (-0.5)
VM = pl.BlockSpec(memory_space=pltpu.VMEM)
SM = pl.BlockSpec(memory_space=pltpu.SMEM)


def sds(shape, dtype=BF):
    return jax.ShapeDtypeStruct(tuple(shape), dtype)


def size_of(a):
    n = jnp.dtype(a.dtype).itemsize
    for d in a.shape:
        n *= d
    return n


def run(body, outs, where, *ins, flops=0, name=None, scratch=()):
    moved = sum(size_of(a) for a in ins) + sum(size_of(o) for o in outs)
    held = moved + sum(size_of(s) for s in scratch)
    return pl.pallas_call(
        body,
        out_shape=list(outs),
        in_specs=[SM] + [VM] * len(ins),
        out_specs=[VM] * len(outs),
        scratch_shapes=[pltpu.VMEM(s.shape, s.dtype) for s in scratch],
        compiler_params=pltpu.CompilerParams(vmem_limit_bytes=min(60 << 20, int(1.25 * held) + (10 << 20))),
        cost_estimate=pl.CostEstimate(flops=flops, bytes_accessed=moved, transcendentals=0),
        name=name,
    )(where, *ins)


T, C, X, Z = 0, 1, 2, 3


class Links:
    def __init__(self, reps, shards):
        self.reps, self.shards = reps, shards
        self.depth = shards // 2
        rank = lax.axis_index("rep")
        shard = lax.axis_index("fsdp")
        self.shard = shard
        self.at = jnp.stack([(rank // 2) % 2, rank % 2, shard % 2, shard // 2]).astype(jnp.int32)

    def core(self, a):
        return lax.ppermute(a, "rep", [(r, r ^ 1) for r in range(self.reps)])

    def y(self, a):
        return lax.ppermute(a, "rep", [(r, r ^ 2) for r in range(self.reps)])

    def rep_bit(self, a, bit):
        return lax.ppermute(a, "rep", [(r, r ^ bit) for r in range(self.reps)])

    def across(self, a):
        return lax.ppermute(a, "fsdp", [(s, s ^ 1) for s in range(self.shards)])

    def along(self, a, k):
        return lax.ppermute(a, "fsdp", [(s, s ^ (2 * k)) for s in range(self.shards)])

    def total(self, a):
        for bit in range(self.reps.bit_length() - 1):
            a = a + self.rep_bit(a, 1 << bit)
        a = a + self.across(a)
        for bit in range(self.depth.bit_length() - 1):
            a = a + self.along(a, 1 << bit)
        return a

    def gather(self, part):
        pieces = [part] + [self.along(part, k) for k in range(1, self.depth)]

        def body(at, *refs):
            out = refs[-1]
            for k in range(self.depth):
                out[at[Z] ^ k] = refs[k][...]

        (column,) = run(body, [sds((self.depth,) + part.shape)], self.at, *pieces, name="column")
        return column, self.across(column)

    def scatter(self, pairs):
        rows, n = pairs[0].shape[-2:]
        depth, count = self.depth, len(pairs)
        pairs = [p.reshape(depth, 2, rows, n) for p in pairs]

        def body1(at, *refs):
            keep, send = refs[-2:]
            for side, out in ((at[X], keep), (1 - at[X], send)):
                for z in range(depth):
                    acc = refs[0][z, side].astype(F32)
                    for r in refs[1:count]:
                        acc = acc + r[z, side].astype(F32)
                    out[z] = acc.astype(BF)

        keep, send = run(body1, [sds((depth, rows, n))] * 2, self.at, *pairs, name="reduce_x")
        got = self.across(send)

        def body2(at, keep, got, *outs):
            for k in range(depth):
                outs[k][...] = (keep[at[Z] ^ k].astype(F32) + got[at[Z] ^ k].astype(F32)).astype(BF)

        pieces = run(body2, [sds((rows, n))] * depth, self.at, keep, got, name="reduce_z")
        parts = [pieces[0]] + [self.along(pieces[k], k) for k in range(1, depth)]

        def body3(at, *refs):
            acc = refs[0][...].astype(F32)
            for r in refs[1:depth]:
                acc = acc + r[...].astype(F32)
            refs[-1][...] = acc.astype(BF)

        (total,) = run(body3, [sds((rows, n))], self.at, *parts, name="reduce_sum")
        for bit in range(2, self.reps.bit_length() - 1):
            total = (total.astype(F32) + self.rep_bit(total, 1 << bit).astype(F32)).astype(BF)
        return total


def mm(a, b):
    return jnp.dot(a, b, preferred_element_type=F32)


def nt(a, b):
    return lax.dot_general(a, b, (((1,), (1,)), ((), ())), preferred_element_type=F32)


def tn(a, b):
    return lax.dot_general(a, b, (((0,), (0,)), ((), ())), preferred_element_type=F32)


def stats(rows):
    mean = jnp.mean(rows, -1, keepdims=True)
    centred = rows - mean
    factor = lax.rsqrt(jnp.mean(centred * centred, -1, keepdims=True) + epsilon)
    return centred * factor, factor


def norm_back(grad, normal, factor, gain):
    scaled = grad * gain
    dx = scaled - jnp.mean(scaled, -1, keepdims=True) - normal * jnp.mean(scaled * normal, -1, keepdims=True)
    return dx * factor, jnp.sum(grad * normal, 0, keepdims=True), jnp.sum(grad, 0, keepdims=True)


def gain_of(ref, i):
    return ref[:, i * D : (i + 1) * D]


def half(i):
    return pl.ds(pl.multiple_of(i * HALF, 128), HALF)


def pair_masks(rows):
    lane = lax.broadcasted_iota(jnp.int32, (rows, 128), 1)
    return lane < HD


def two_heads(a):
    first = pair_masks(a.shape[0])
    zero = jnp.zeros_like(a)
    return jnp.concatenate([jnp.where(first, a, zero), jnp.where(first, zero, a)], 0)


def one_pair(a):
    n = a.shape[0] // 2
    return jnp.where(pair_masks(n), a[:n], a[n:])


def softmax(scores):
    peak = jnp.max(scores, -1, keepdims=True)
    expo = jnp.exp(scores - peak)
    total = jnp.sum(expo, -1, keepdims=True)
    return expo / total, peak + jnp.log(total)


def pack_a(at, query, keyval, gains, biases, part):
    rows, size = query.shape[0], gains.shape[1]
    part[:rows, :HALF] = keyval[:, pl.ds(pl.multiple_of(at[T] * D + at[C] * HALF, 128), HALF)]
    part[:rows, HALF:] = query[:, half(at[C])]
    part[rows:, :] = jnp.zeros((16, D), BF)
    g, b = gains[...], biases[...]
    g_hi, b_hi = g.astype(BF), b.astype(BF)
    g_lo, b_lo = (g - g_hi.astype(F32)).astype(BF), (b - b_hi.astype(F32)).astype(BF)
    row = lax.broadcasted_iota(jnp.int32, (16, size), 0)
    out = jnp.zeros((16, size), F32)
    for i, v in enumerate((g_hi, g_lo, b_hi, b_lo)):
        out = jnp.where(row == i, jnp.broadcast_to(v.astype(F32), (16, size)), out)
    part[rows:, :size] = out.astype(BF)


def pack_rest(at, output, gate, qkv, self_out, up, down, part_bc, part_d):
    rows = output.shape[0]
    shards = D // rows
    t0, c0 = at[T] == 0, at[C] == 0
    gate_c, out_c, self_c = gate[:, half(at[C])], output[:, half(at[C])], self_out[:, half(at[C])]
    part_bc[:, :HALF] = jnp.where(t0, gate_c[:rows], gate_c[rows:])
    part_bc[:, HALF:D] = jnp.where(t0, out_c, self_c)
    pieces = []
    for i in range(3):
        v = qkv[:, pl.ds(pl.multiple_of(i * D + at[T] * HALF, 128), HALF)]
        pieces.append(jnp.where(c0, v[:, :QUART], v[:, QUART:]))
    part_bc[:, D:] = jnp.concatenate(pieces, 1)
    pieces = []
    for s in range(shards):
        v = [up[:, (s * 4 + g) * rows : (s * 4 + g + 1) * rows] for g in range(4)]
        pieces.append(jnp.where(t0, jnp.where(c0, v[0], v[1]), jnp.where(c0, v[2], v[3])))
    part_d[:, :D] = jnp.concatenate(pieces, 1)
    v = [down[g * rows : (g + 1) * rows, :] for g in range(4)]
    part_d[:, D:] = jnp.where(t0, jnp.where(c0, v[0], v[1]), jnp.where(c0, v[2], v[3]))


def join_a(rows, size, at, mine, other, kv, q, gains, biases):
    depth = mine.shape[0]
    for src, side in ((mine, at[X]), (other, 1 - at[X])):
        for z in range(depth):
            kv[z, side] = src[z, :rows, :HALF]
            q[z, side] = src[z, :rows, HALF:]
    first = at[X] == 0
    for z in range(depth):
        a, b = mine[z, rows:, :size].astype(F32), other[z, rows:, :size].astype(F32)
        for i, v in enumerate((jnp.where(first, a, b), jnp.where(first, b, a))):
            s = (z * 2 + i) * size
            gains[:, s : s + size] = v[0:1] + v[1:2]
            biases[:, s : s + size] = v[2:3] + v[3:4]


def join_bc(at, mine, other, b, c):
    depth = mine.shape[0]
    for src, side in ((mine, at[X]), (other, 1 - at[X])):
        for z in range(depth):
            b[z, side] = src[z, :, :D]
            c[z, side] = src[z, :, D:]


def join_d(at, mine, other, out):
    for src, side in ((mine, at[X]), (other, 1 - at[X])):
        for z in range(mine.shape[0]):
            out[z, side] = src[z]


def place_b(at, oo, oc, to, tc, cross_out, self_out, gate):
    t, c = at[T], at[C]
    for src, tt, cc in ((oo, t, c), (oc, t, 1 - c), (to, 1 - t, c), (tc, 1 - t, 1 - c)):
        for s in range(src.shape[0]):
            gate[s, tt, :, half(cc)] = src[s, :, :HALF]

        @pl.when(tt == 0)
        def _():
            cross_out[:, :, half(cc)] = src[:, :, HALF:]

        @pl.when(tt == 1)
        def _():
            self_out[:, :, half(cc)] = src[:, :, HALF:]


def keyval_kernel(at, text, visual, gains, biases, oo, oc, to, tc, q_own, q_oth,
                  text_normed, kv, w_kv, w_q, normed, queries):
    t, c = at[T], at[C]

    @pl.when(pl.program_id(0) == 0)
    def _():
        for src, tt, cc in ((oo, t, c), (oc, t, 1 - c), (to, 1 - t, c), (tc, 1 - t, 1 - c)):
            w_kv[:, pl.ds(pl.multiple_of(tt * D + cc * HALF, 128), HALF)] = src[...]
        w_q[:, half(c)] = q_own[...]
        w_q[:, half(1 - c)] = q_oth[...]
        normal, _f = stats(visual[...].astype(F32))
        n = (normal * gain_of(gains, 0) + gain_of(biases, 0)).astype(BF)
        normed[...] = n
        queries[...] = mm(n, w_q[...]).astype(BF)

    normal, _f = stats(text[...].astype(F32))
    n = (normal * gain_of(gains, 1) + gain_of(biases, 1)).astype(BF)
    text_normed[...] = n
    kv[...] = mm(n, w_kv[...]).astype(BF)


def cross_bias(owner, valid):
    n, m = valid.shape[1], owner.shape[1]
    parent = owner[...] == lax.broadcasted_iota(jnp.int32, (n, m), 0)
    ones = jnp.where(parent, 1.0, 0.0).astype(BF)
    real = jnp.broadcast_to(valid[...].astype(F32), (8, n)).astype(BF)
    present = mm(real, ones)[0:1] > 0.5
    return jnp.where(parent, shared_sheet_reward, 0.0) + jnp.where(present, 0.0, filtered_logits)


def cross_fwd(owner, valid, q, k, v, out, logs, bias):
    @pl.when(pl.program_id(0) == 0)
    def _():
        bias[...] = cross_bias(owner, valid)

    b = bias[...]
    scores = nt(two_heads(q[...]), k[...]) * SCALE + jnp.concatenate([b, b], 0)
    weight, log = softmax(scores)
    logs[0] = log
    out[...] = one_pair(mm(weight.astype(BF), v[...])).astype(BF)


def gate_kernel(at, mixed, normed, visual, gains, biases, w_out, w_gate, cross, gate, joined, second):
    rows = mm(mixed[...], w_out[...]).astype(BF)
    cross[...] = rows
    g = jax.nn.sigmoid(mm(normed[...], w_gate[:D]) + mm(rows, w_gate[D:]))
    gate[...] = g
    j = visual[...].astype(F32) + g * rows.astype(F32)
    joined[...] = j
    normal, _f = stats(j)
    second[...] = (normal * gain_of(gains, 2) + gain_of(biases, 2)).astype(BF)


def head_order(at, a):
    return jnp.where(at[C] == 0, a, jnp.concatenate([a[:, QUART:], a[:, :QUART]], 1))


def self_bias(valid):
    return jnp.where(valid > 0.5, 0.0, filtered_logits)


def self_fwd(at, second0, second1, valid0, valid1, w_own, w_oth, triple, att0, att1):
    n = second0.shape[0]
    rows = jnp.concatenate([second0[...], second1[...]], 0)
    own, oth = mm(rows, w_own[...]).astype(BF), mm(rows, w_oth[...]).astype(BF)
    for i in range(3):
        triple[:, i * HALF : (i + 1) * HALF] = jnp.concatenate(
            [own[:, i * QUART : (i + 1) * QUART], oth[:, i * QUART : (i + 1) * QUART]], 1)
    for page, (valid, att) in enumerate(((valid0, att0), (valid1, att1))):
        bias = self_bias(valid[...])
        r = slice(page * n, (page + 1) * n)
        outs = []
        for p in range(3):
            q, k, v = [triple[r, i * HALF + p * 128 : i * HALF + (p + 1) * 128] for i in range(3)]
            weight, _l = softmax(nt(two_heads(q), k) * SCALE + bias)
            outs.append(one_pair(mm(weight.astype(BF), v)).astype(BF))
        att[...] = head_order(at, jnp.concatenate(outs, 1))


def carry_kernel(at, mine, came, joined, gains, biases, w, attended, carried, third):
    attended[:, half(at[T])] = mine[...]
    attended[:, half(1 - at[T])] = came[...]
    c = joined[...] + mm(attended[...], w[...])
    carried[...] = c
    normal, _f = stats(c)
    third[...] = (normal * gain_of(gains, 3) + gain_of(biases, 3)).astype(BF)


def ffn_kernel(last, at, third0, third1, cot0, cot1, w, *refs):
    n = third0.shape[0]
    if last:
        y0i, y1i, d0i, d1i, y0, y1, d0, d1, grad = refs
    else:
        y0, y1, d0, d1, grad = refs
    rows = jnp.concatenate([third0[...], third1[...]], 0)
    cot = jnp.concatenate([cot0[...], cot1[...]], 0)
    up, down = w[:, :D], w[:, D:]
    v = mm(rows, up)
    k = (2.0 / 3.141592653589793) ** 0.5
    th = jnp.tanh(k * (v + 0.044715 * (v * v * v)))
    act = (0.5 * v * (1.0 + th)).astype(BF)
    slope = 0.5 * (1.0 + th) + 0.5 * v * (1.0 - th * th) * (k * (1.0 + 3.0 * 0.044715 * (v * v)))
    y = mm(act, down)
    grad[:, D:] = tn(act, cot).astype(BF)
    dl = (nt(cot, down) * slope).astype(BF)
    d = nt(dl, up)
    grad[:, :D] = tn(rows, dl).astype(BF)
    if last:
        y0[...] = y[:n] + y0i[...]
        y1[...] = (y[n:] + y1i[...]).astype(BF)
        d0[...] = d[:n] + d0i[...]
        d1[...] = (d[n:] + d1i[...]).astype(BF)
    else:
        y0[...], y1[...], d0[...], d1[...] = y[:n], y[n:], d[:n], d[n:]


def carry_back(at, d0, came, carried, cot, attended, gains, w, d_carried, mine, send, grad, sums):
    normal, factor = stats(carried[...])
    dx, gain, bias = norm_back(d0[...] + came[...].astype(F32), normal, factor, gain_of(gains, 3))
    dc = cot[...].astype(F32) + dx
    d_carried[...] = dc
    low = dc.astype(BF)
    da = nt(low, w[...]).astype(BF)
    t0 = at[T] == 0
    mine[...] = head_order(at, jnp.where(t0, da[:, :HALF], da[:, HALF:]))
    send[...] = head_order(at, jnp.where(t0, da[:, HALF:], da[:, :HALF]))
    grad[...] = tn(attended[...], low).astype(BF)
    sums[0:1], sums[1:2] = gain, bias


def self_back(at, triple, da0, da1, valid0, valid1, second0, second1, w_own, w_oth, d0, d1, g_own, g_oth, dt):
    n = second0.shape[0]
    for page, (valid, da) in enumerate(((valid0, da0), (valid1, da1))):
        bias = self_bias(valid[...])
        r = slice(page * n, (page + 1) * n)
        for p in range(3):
            q, k, v = [triple[r, i * HALF + p * 128 : i * HALF + (p + 1) * 128] for i in range(3)]
            qq = two_heads(q)
            dd = two_heads(da[:, p * 128 : (p + 1) * 128])
            weight, _l = softmax(nt(qq, k) * SCALE + bias)
            dp = nt(dd, v)
            ds = (weight * (dp - jnp.sum(weight * dp, -1, keepdims=True))).astype(BF)
            grads = (one_pair(mm(ds, k)) * SCALE, tn(ds, qq) * SCALE, tn(weight.astype(BF), dd))
            for i in range(3):
                dt[r, i * HALF + p * 128 : i * HALF + (p + 1) * 128] = grads[i].astype(BF)
    own = jnp.concatenate([dt[:, i * HALF : i * HALF + QUART] for i in range(3)], 1)
    oth = jnp.concatenate([dt[:, i * HALF + QUART : (i + 1) * HALF] for i in range(3)], 1)
    rows = jnp.concatenate([second0[...], second1[...]], 0)
    g_own[...] = tn(rows, own).astype(BF)
    g_oth[...] = tn(rows, oth).astype(BF)
    d = nt(own, w_own[...]) + nt(oth, w_oth[...])
    d0[...] = d[:n]
    d1[...] = d[n:].astype(BF)


def gate_back(at, d_carried, d0, came, joined, normed, cross, gate, mixed, gains, w_gate, w_out, g_self,
              d_joined, d_mixed, d_normed, keep, send, sums):
    t, c = at[T], at[C]
    rows = keep.shape[2]
    normal, factor = stats(joined[...])
    dx, gain, bias = norm_back(d0[...] + came[...].astype(F32), normal, factor, gain_of(gains, 2))
    dj = d_carried[...] + dx
    d_joined[...] = dj
    sums[0:1], sums[1:2] = gain, bias
    g = gate[...]
    dg = (dj * cross[...].astype(F32) * g * (1.0 - g)).astype(BF)
    d_normed[...] = nt(dg, w_gate[:D])
    dc = (dj * g + nt(dg, w_gate[D:])).astype(BF)
    d_mixed[...] = nt(dc, w_out[...]).astype(BF)
    g_gate = jnp.concatenate([tn(normed[...], dg).astype(BF), tn(cross[...], dg).astype(BF)], 0)
    g_gate = g_gate.reshape(D // rows, 2, rows, D)
    g_out = tn(mixed[...], dc).astype(BF).reshape(D // rows, rows, D)
    g_so = g_self[...].reshape(D // rows, rows, D)
    for tt in range(2):
        for cc in range(2):
            lanes = slice(cc * HALF, (cc + 1) * HALF)
            side = g_out if tt == 0 else g_so
            for out, same in ((keep, True), (send, False)):
                @pl.when((c == cc) == same)
                def _():
                    out[t ^ tt, :, :, :HALF] = g_gate[:, tt, :, lanes]
                    out[t ^ tt, :, :, HALF:] = side[:, :, lanes]


def cross_back(owner, valid, q, k, v, dm, logs, dq, dkv, bias):
    @pl.when(pl.program_id(0) == 0)
    def _():
        bias[...] = cross_bias(owner, valid)

    b = bias[...]
    qq, dd = two_heads(q[...]), two_heads(dm[...])
    scores = nt(qq, k[...]) * SCALE + jnp.concatenate([b, b], 0)
    weight = jnp.exp(scores - logs[0])
    dp = nt(dd, v[...])
    ds = (weight * (dp - jnp.sum(weight * dp, -1, keepdims=True))).astype(BF)
    dq[...] = (one_pair(mm(ds, k[...])) * SCALE).astype(BF)
    dkv[0] = (tn(ds, qq) * SCALE).astype(BF)
    dkv[1] = tn(weight.astype(BF), dd).astype(BF)


def cross_weights(at, text_normed, normed, dq, dkv, grad):
    t = at[T]
    x = text_normed[...]
    grad[t] = tn(x, dkv[0]).astype(BF)
    grad[1 - t] = tn(x, dkv[1]).astype(BF)
    grad[2] = tn(normed[...], dq[...]).astype(BF)


def text_back(at, text, gains, w_kv, own, oth, grad, sums):
    c = at[C]
    d = nt(own[0], w_kv[:, half(c)])
    d = d + nt(oth[0], w_kv[:, half(1 - c)])
    d = d + nt(own[1], w_kv[:, pl.ds(pl.multiple_of(D + c * HALF, 128), HALF)])
    d = d + nt(oth[1], w_kv[:, pl.ds(pl.multiple_of(D + (1 - c) * HALF, 128), HALF)])
    normal, factor = stats(text[...].astype(F32))
    dx, gain, bias = norm_back(d, normal, factor, gain_of(gains, 1))
    grad[...] = dx

    @pl.when(pl.program_id(0) == 0)
    def _():
        sums[...] = jnp.zeros_like(sums)

    sums[0:1] += gain
    sums[1:2] += bias


def visual_back(at, d_normed, dq_own, dq_oth, w_q, visual, d_joined, gains, s1, s2, s3, grad, sums):
    c = at[C]
    d = d_normed[...] + nt(dq_own[...], w_q[:, half(c)]) + nt(dq_oth[...], w_q[:, half(1 - c)])
    normal, factor = stats(visual[...].astype(F32))
    dx, gain, bias = norm_back(d, normal, factor, gain_of(gains, 0))
    grad[...] = d_joined[...] + dx
    for i, (g, b) in enumerate(((gain, bias), (s1[0:1], s1[1:2]), (s2[0:1], s2[1:2]), (s3[0:1], s3[1:2]))):
        sums[i : i + 1], sums[i + 4 : i + 5] = g, b


def finish_a(at, r, ry, rc, ryc, g_query, g_keyval):
    t, c = at[T], at[C]
    for a, b, cc in ((r, ry, c), (rc, ryc, 1 - c)):
        g_keyval[:, pl.ds(pl.multiple_of(t * D + cc * HALF, 128), HALF)] = a[:, :HALF].astype(F32)
        g_keyval[:, pl.ds(pl.multiple_of((1 - t) * D + cc * HALF, 128), HALF)] = b[:, :HALF].astype(F32)
        g_query[:, half(cc)] = a[:, HALF:].astype(F32) + b[:, HALF:].astype(F32)


def finish_bcd(at, *refs):
    groups, (g_out, g_gate, g_self, g_qkv, g_up, g_down) = refs[:12], refs[12:]
    t, c = at[T], at[C]
    rows = g_out.shape[0]
    shards = D // rows
    t0, c0 = t == 0, c == 0
    b, cq, d = groups[0:4], groups[4:8], groups[8:12]

    def order(g, rs, ls):
        own, y, core, both = [r[rs, ls].astype(F32) for r in g]
        a0, a1 = jnp.where(c0, own, core), jnp.where(c0, core, own)
        b0, b1 = jnp.where(c0, y, both), jnp.where(c0, both, y)
        return jnp.where(t0, a0, b0), jnp.where(t0, a1, b1), jnp.where(t0, b0, a0), jnp.where(t0, b1, a1)

    every = slice(None)
    p = order(b, every, slice(0, HALF))
    for i in range(4):
        g_gate[(i // 2) * rows : (i // 2 + 1) * rows, (i % 2) * HALF : (i % 2 + 1) * HALF] = p[i]
    p = order(b, every, slice(HALF, D))
    g_out[...] = jnp.concatenate(p[:2], 1)
    g_self[...] = jnp.concatenate(p[2:], 1)
    for i in range(3):
        p = order(cq, every, slice(i * QUART, (i + 1) * QUART))
        g_qkv[:, i * D : (i + 1) * D] = jnp.concatenate(p, 1)
    for s in range(shards):
        p = order(d, every, slice(s * rows, (s + 1) * rows))
        g_up[:, s * 4 * rows : (s + 1) * 4 * rows] = jnp.concatenate(p, 1)
    p = order(d, every, slice(D, 2 * D))
    for i in range(4):
        g_down[i * rows : (i + 1) * rows] = p[i]


def local(reps, shards, visual, text, visual_valid, block_owner, cross_query, cross_keyval, cross_output, gate_weight,
          self_qkv, self_output, ffn_up, ffn_down, norm_gains, norm_biases, cotangent):
    ln = Links(reps, shards)
    at = ln.at
    visual, text, cotangent = visual[0], text[0], cotangent[0]
    rows, size = cross_query.shape[0], norm_gains.shape[0]
    vis, txt = visual.shape[0], text.shape[0]
    depth = shards // 2
    split = (depth, 2, rows)

    (part_a,) = run(pack_a, [sds((rows + 16, D))], at, cross_query, cross_keyval,
                    norm_gains.reshape(1, size), norm_biases.reshape(1, size), name="pack_a")
    mine, other = ln.gather(part_a)
    kv_oo, q_own, gains, biases = run(
        functools.partial(join_a, rows, size),
        [sds(split + (HALF,)), sds(split + (HALF,)), sds((1, 4 * D), F32), sds((1, 4 * D), F32)],
        at, mine, other, name="join_a")
    kv_oo, q_own = kv_oo.reshape(D, HALF), q_own.reshape(D, HALF)
    kv_to = ln.y(kv_oo)
    kv_oc, q_oth, kv_tc = ln.core(kv_oo), ln.core(q_own), ln.core(kv_to)

    part_bc, part_d = run(pack_rest, [sds((rows, D + 3 * QUART)), sds((rows, 2 * D))], at,
                          cross_output, gate_weight, self_qkv, self_output, ffn_up, ffn_down, name="pack_rest")
    b_oo, c_own = run(join_bc, [sds(split + (D,)), sds(split + (3 * QUART,))], at, *ln.gather(part_bc), name="join_bc")
    b_oo, c_own = b_oo.reshape(shards, rows, D), c_own.reshape(D, 3 * QUART)
    b_to = ln.y(b_oo)
    b_oc, b_tc, c_oth = ln.core(b_oo), ln.core(b_to), ln.core(c_own)
    w_out, w_self, w_gate = run(
        place_b, [sds((shards, rows, D)), sds((shards, rows, D)), sds((shards, 2, rows, D))],
        at, b_oo, b_oc, b_to, b_tc, name="place_b")
    w_out, w_self, w_gate = w_out.reshape(D, D), w_self.reshape(D, D), w_gate.reshape(2 * D, D)
    (d_own,) = run(join_d, [sds(split + (2 * D,))], at, *ln.gather(part_d), name="join_d")
    d_own = d_own.reshape(D, 2 * D)
    d_oth = ln.core(d_own)

    valid = visual_valid.astype(F32)
    valid_y, cot_y = ln.y(valid), ln.y(cotangent)

    def whole(shape):
        return pl.BlockSpec(shape, lambda *_: (0,) * len(shape))

    def grid_run(body, grid, in_specs, outs, out_specs, *ins, scratch=(), flops=0, name=None, vmem=40):
        return pl.pallas_call(
            body, grid=grid, in_specs=in_specs, out_specs=out_specs, out_shape=outs,
            scratch_shapes=[pltpu.VMEM(s.shape, s.dtype) for s in scratch],
            compiler_params=pltpu.CompilerParams(vmem_limit_bytes=vmem << 20),
            cost_estimate=pl.CostEstimate(flops=flops, transcendentals=0,
                                          bytes_accessed=sum(size_of(a) for a in ins) + sum(size_of(o) for o in outs)),
            name=name)(*ins)

    tile = txt // 5
    row_tile = pl.BlockSpec((tile, D), lambda i: (i, 0))
    text_normed, kv, w_kv, w_q, normed, queries = grid_run(
        keyval_kernel, (5,),
        [SM, row_tile, whole((vis, D)), whole((1, 4 * D)), whole((1, 4 * D))] + [whole((D, HALF))] * 6,
        [sds((txt, D)), sds((txt, 2 * D)), sds((D, 2 * D)), sds((D, D)), sds((vis, D)), sds((vis, D))],
        [row_tile, pl.BlockSpec((tile, 2 * D), lambda i: (i, 0)), whole((D, 2 * D)), whole((D, D)), whole((vis, D)), whole((vis, D))],
        at, text, visual, gains, biases, kv_oo, kv_oc, kv_to, kv_tc, q_own, q_oth,
        flops=2 * (txt * 2 + vis) * D * D, name="keyval")
    pairs = H // 2
    col = lambda n, off=0, k=0: pl.BlockSpec((n, 128), lambda p: (0, p + off))
    mixed, logs = grid_run(
        cross_fwd, (pairs,),
        [whole((1, txt)), whole((1, vis)), col(vis), col(txt), col(txt, pairs)],
        [sds((vis, D)), sds((pairs, 2 * vis, 1), F32)],
        [col(vis), pl.BlockSpec((1, 2 * vis, 1), lambda p: (p, 0, 0))],
        block_owner, visual_valid, queries, kv, kv, scratch=[sds((vis, txt), F32)],
        flops=8 * vis * txt * D, name="cross_fwd")
    cross, gate, joined, second = run(
        gate_kernel, [sds((vis, D)), sds((vis, D), F32), sds((vis, D), F32), sds((vis, D))],
        at, mixed, normed, visual, gains, biases, w_out, w_gate, flops=6 * vis * D * D, name="gate")
    second_y = ln.y(second)
    triple, att_mine, att_send = run(
        self_fwd, [sds((2 * vis, 3 * HALF)), sds((vis, HALF)), sds((vis, HALF))],
        at, second, second_y, valid, valid_y, c_own, c_oth, flops=8 * vis * D * D, name="self_fwd")
    attended, carried, third = run(
        carry_kernel, [sds((vis, D)), sds((vis, D), F32), sds((vis, D))],
        at, att_mine, ln.y(att_send), joined, gains, biases, w_self, flops=2 * vis * D * D, name="carry")
    third_y = ln.y(third)

    page = sds((vis, D), F32)
    y0, y1, d0, d1, grad_d_oth = run(
        functools.partial(ffn_kernel, False), [page] * 4 + [sds((D, 2 * D))],
        at, third, third_y, cotangent, cot_y, d_oth, flops=24 * vis * D * D, name="ffn_first")
    grad_d_came = ln.core(grad_d_oth)
    y0, y1, d0, d1, grad_d = run(
        functools.partial(ffn_kernel, True), [page, sds((vis, D))] * 2 + [sds((D, 2 * D))],
        at, third, third_y, cotangent, cot_y, d_own, y0, y1, d0, d1, flops=24 * vis * D * D, name="ffn_second")
    d1 = ln.y(d1)
    layer_out = (carried + y0 + ln.y(y1).astype(F32)).astype(BF)
    sum_d = ln.scatter([g.reshape(shards, rows, 2 * D) for g in (grad_d, grad_d_came)])

    d_carried, da_mine, da_send, g_self, sums3 = run(
        carry_back, [page, sds((vis, HALF)), sds((vis, HALF)), sds((D, D)), sds((2, D), F32)],
        at, d0, d1, carried, cotangent, attended, gains, w_self, flops=4 * vis * D * D, name="carry_back")
    ds0, ds1, g_c_own, g_c_oth = run(
        self_back, [page, sds((vis, D)), sds((D, 3 * QUART)), sds((D, 3 * QUART))],
        at, triple, da_mine, ln.y(da_send), valid, valid_y, second, second_y, c_own, c_oth,
        scratch=[sds((2 * vis, 3 * HALF))], flops=16 * vis * D * D, name="self_back")
    g_c_came = ln.core(g_c_oth)
    d_joined, d_mixed, d_normed, b_keep, b_send, sums2 = run(
        gate_back, [page, sds((vis, D)), page, sds((2, shards, rows, D)), sds((2, shards, rows, D)), sds((2, D), F32)],
        at, d_carried, ds0, ln.y(ds1), joined, normed, cross, gate, mixed, gains, w_gate, w_out, g_self,
        flops=12 * vis * D * D, name="gate_back")
    sum_c = ln.scatter([g.reshape(shards, rows, 3 * QUART) for g in (g_c_own, g_c_came)])

    def add_core(keep, came):
        def body(at, keep, came, *outs):
            for i, out in enumerate(outs):
                out[...] = (keep[i].astype(F32) + came[i].astype(F32)).astype(BF)

        return run(body, [sds(keep.shape[1:])] * keep.shape[0], at, keep, came, name="add_core")

    own_b, oth_b = add_core(b_keep, ln.core(b_send))
    sum_b = ln.scatter([own_b, ln.y(oth_b)])

    def back_half(index):
        def spec(n, off=0):
            return pl.BlockSpec((n, 128), lambda p, at: (0, (at[C] ^ index) * 3 + p + off))

        fixed = lambda shape: pl.BlockSpec(shape, lambda p, at: (0,) * len(shape))
        ins = (at, block_owner, visual_valid, queries, kv, kv, d_mixed, logs)
        outs = [sds((vis, HALF)), sds((2, txt, HALF))]
        return pl.pallas_call(
            lambda at, *refs: cross_back(*refs),
            grid_spec=pltpu.PrefetchScalarGridSpec(
                num_scalar_prefetch=1, grid=(3,),
                in_specs=[fixed((1, txt)), fixed((1, vis)), spec(vis), spec(txt), spec(txt, pairs), spec(vis),
                          pl.BlockSpec((1, 2 * vis, 1), lambda p, at: ((at[C] ^ index) * 3 + p, 0, 0))],
                out_specs=[pl.BlockSpec((vis, 128), lambda p, at: (0, p)),
                           pl.BlockSpec((2, txt, 128), lambda p, at: (0, 0, p))],
                scratch_shapes=[pltpu.VMEM((vis, txt), F32)]),
            out_shape=outs,
            compiler_params=pltpu.CompilerParams(vmem_limit_bytes=30 << 20),
            cost_estimate=pl.CostEstimate(flops=10 * vis * txt * D, transcendentals=0,
                                          bytes_accessed=sum(size_of(a) for a in ins) + sum(size_of(o) for o in outs)),
            name="cross_back")(*ins)

    def weights_half(dq, dkv):
        (grad,) = run(cross_weights, [sds((3, D, HALF))], at, text_normed, normed, dq, dkv,
                      flops=2 * txt * D * D, name="cross_weights")
        return grad

    dq_oth, dkv_oth = back_half(1)
    a_send = weights_half(dq_oth, dkv_oth)
    a_came = ln.core(a_send)
    dq_own, dkv_own = back_half(0)
    a_keep = weights_half(dq_own, dkv_own)

    def add_a(at, keep, came, own, oth):
        own[:, :HALF] = (keep[0].astype(F32) + came[0].astype(F32)).astype(BF)
        own[:, HALF:] = (keep[2].astype(F32) + came[2].astype(F32)).astype(BF)
        oth[...] = (keep[1].astype(F32) + came[1].astype(F32)).astype(BF)

    own_a, oth_a = run(add_a, [sds((D, D)), sds((D, HALF))], at, a_keep, a_came, name="add_a")
    oth_a = ln.y(oth_a)

    def add_y(at, own, came, out):
        out[:, :HALF] = (own[:, :HALF].astype(F32) + came[...].astype(F32)).astype(BF)
        out[:, HALF:] = own[:, HALF:]

    (own_a,) = run(add_y, [sds((D, D))], at, own_a, oth_a, name="add_y")
    sum_a = ln.scatter([own_a.reshape(shards, rows, D)])

    row3 = pl.BlockSpec((2, tile, HALF), lambda i: (0, i, 0))
    grad_text, sums1 = grid_run(
        text_back, (5,), [SM, row_tile, whole((1, 4 * D)), whole((D, 2 * D)), row3, row3],
        [sds((txt, D), F32), sds((2, D), F32)], [row_tile, whole((2, D))],
        at, text, gains, w_kv, dkv_own, dkv_oth, flops=4 * txt * D * D, name="text_back")
    grad_visual, sums = run(
        visual_back, [page, sds((8, D), F32)],
        at, d_normed, dq_own, dq_oth, w_q, visual, d_joined, gains, sums1, sums2, sums3, flops=2 * vis * D * D, name="visual_back")
    sums = ln.total(sums).reshape(2, shards, size)
    sums = lax.dynamic_index_in_dim(sums, ln.shard, 1, False)

    def groups(r):
        ry = ln.y(r)
        return r, ry, ln.core(r), ln.core(ry)

    out = lambda r, n: sds((r, n), F32)
    g_out, g_gate, g_self_out, g_qkv, g_up, g_down = run(
        finish_bcd,
        [out(rows, D), out(2 * rows, D), out(rows, D), out(rows, 3 * D), out(rows, 4 * D), out(4 * rows, D)],
        at, *groups(sum_b), *groups(sum_c), *groups(sum_d), name="finish_bcd")
    g_query, g_keyval = run(finish_a, [out(rows, D), out(rows, 2 * D)], at, *groups(sum_a), name="finish_a")
    return (layer_out[None], grad_visual[None], grad_text[None], g_query, g_keyval, g_out, g_gate, g_qkv, g_self_out,
            g_up, g_down, sums[0], sums[1])


def solution(mesh):
    pages = P(("rep", "fsdp"), None, None)
    flags = P(("rep", "fsdp"), None)
    matrix = P("fsdp", None)
    vector = P("fsdp")
    in_specs = (pages, pages, flags, flags) + (matrix,) * 8 + (vector, vector, pages)
    out_specs = (pages, pages, pages) + (matrix,) * 8 + (vector, vector)
    reps, shards = mesh.shape["rep"], mesh.shape["fsdp"]

    def program(*args):
        return local(reps, shards, *args)

    return jax.shard_map(program, mesh=mesh, in_specs=in_specs, out_specs=out_specs, check_vma=False)
```

time: 559 us -> 422 us (0.75)
  matrix products: 116 us -> 0 us
  Pallas kernels: 0 us -> 106 us
  local copies, waits for them, and re-layouts: 134 us -> 41.6 us
  waiting for transfers between devices: 104 us -> 194 us
  other arithmetic: 82.1 us -> 2.28 us
  starting transfers between devices: 112 us -> 69.1 us
    dot_general x71 -> x0, matrix products: 116 us -> none  [the longest x18 36 us: mm_nt(): lax.dot_general(a, b, (((1,), (1,)), ((), ())), preferred_element_type=F32)]
    pallas_call x0 -> x42, Pallas kernels: none -> 106 us  [the longest x37 70.2 us: run(): pl.pallas_call(body, out_shape=list(outs), in_specs=[SM] + [VM] * len(ins...]
    ppermute x26 -> x23, waiting for transfers between devices: 57 us -> 109 us  [along(): return lax.ppermute(a, 'fsdp', [(s, s ^ 2 * k) for s in range(self.shards)])]
    another operation x34 -> x1, other arithmetic: 29 us -> 0.08 us  [__init__(): jnp.stack([rank // 2 % 2, rank % 2, shard % 2, shard // 2])]
    ppermute x12 -> x19, starting transfers between devices: 48.7 us -> 21.7 us  [core(): return lax.ppermute(a, 'rep', [(r, r ^ 1) for r in range(self.reps)])]
    convert_element_type x25 -> x1, other arithmetic: 22 us -> 0.51 us  [local(): valid = visual_valid.astype(F32)]
    ppermute x17, waiting for transfers between devices: 28.5 us -> 49.2 us  [y(): return lax.ppermute(a, 'rep', [(r, r ^ 2) for r in range(self.reps)])]
    another operation x20 -> x0, local copies, waits for them, and re-layouts: 19 us -> none  [the longest x4 6.21 us: local(): triple = jnp.stack(triple, 3).reshape(2, vis, 3, 2 * w3)]
  transfers between devices with their start and end apart: 66 -> 69, of which waited for: 27 -> 29; matrix products, arithmetic and copies ran while one was open for 57% -> 2% of each run, Pallas kernels for 0% -> 19%
where the time goes in v2:
time: 422 us; the launch traced here: 415 us
  waiting for transfers between devices  194 us (46%)
  Pallas kernels  106 us (25%)
  starting transfers between devices  69.1 us (16%)
  local copies, waits for them, and re-layouts  41.6 us (10%)
    ppermute x23, waiting for transfers between devices, along(): return lax.ppermute(a, 'fsdp', [(s, s ^ 2 * k) for s in range(self.shards)])  109 us
    pallas_call x37, Pallas kernels, run(): pl.pallas_call(body, out_shape=list(outs), in_specs=[SM] + [VM] * len(ins...  70.2 us
    ppermute x17, waiting for transfers between devices, y(): return lax.ppermute(a, 'rep', [(r, r ^ 2) for r in range(self.reps)])  49.2 us
    unnamed x200, local copies, waits for them, and re-layouts  33.6 us
    ppermute x8, waiting for transfers between devices, across(): return lax.ppermute(a, 'fsdp', [(s, s ^ 1) for s in range(self.shards)])  30.5 us
    ppermute x23, starting transfers between devices, along(): return lax.ppermute(a, 'fsdp', [(s, s ^ 2 * k) for s in range(self.shards)])  26 us
    pallas_call x3, Pallas kernels, grid_run(): pl.pallas_call(body, grid=grid, in_specs=in_specs, out_specs=out_specs, o...  23.8 us
    ppermute x19, starting transfers between devices, core(): return lax.ppermute(a, 'rep', [(r, r ^ 1) for r in range(self.reps)])  21.7 us
  transfers between devices with their start and end apart: 69, of which 29 were waited for; matrix products, arithmetic and copies ran while one was open for 2% of the time, Pallas kernels for 19%

profile of v2, /device:TPU:1, one launch (start us, length us, event | category | flops | bytes accessed | tf_op | source)
XLA Modules:
  0.0 415.0 jit_solution(8726507072783737202)
XLA Ops:
  8.2 4.2 %collective-permute-start.10 = (bf16[96,1344]{1,0:T(8,128)(2,1)S(1)}, bf16[96,1344]{1,0:T(8,128)(2,1)S(1)}, u32[]{:S(2)}, u32[]{:S(2)}) collective-permute-start(bf16[96,1344]{1,0:T(8,128)(2,1)S(1)} %get-tuple-element.119.refs_0_), channel_id=1, source_target_pairs={{0,6},{1,7},{2,4},{3,5},{4,2},{5,3},{6,0},{7,1},{8,14},{9,15},{10,... | collective-permute-start | bytes 774152 | tf_op jit(solution)/shard_map/ppermute | solution.py:77
  12.8 5.9 %collective-permute-done.10.refs_3_ = bf16[96,1344]{1,0:T(8,128)(2,1)S(1)} collective-permute-done((bf16[96,1344]{1,0:T(8,128)(2,1)S(1)}, bf16[96,1344]{1,0:T(8,128)(2,1)S(1)}, u32[]{:S(2)}, u32[]{:S(2)}) %collective-permute-start.10) | collective-permute-done | bytes 258080 | tf_op jit(solution)/shard_map/ppermute | solution.py:77
  18.7 16.3 %collective-permute-done.9.refs_2_ = bf16[96,1344]{1,0:T(8,128)(2,1)S(1)} collective-permute-done((bf16[96,1344]{1,0:T(8,128)(2,1)S(1)}, bf16[96,1344]{1,0:T(8,128)(2,1)S(1)}, u32[]{:S(2)}, u32[]{:S(2)}) %collective-permute-start.9) | collective-permute-done | bytes 258080 | tf_op jit(solution)/shard_map/ppermute | solution.py:77
  40.6 5.2 %collective-permute-done.23.refs_3_ = bf16[96,1536]{1,0:T(8,128)(2,1)S(1)} collective-permute-done((bf16[96,1536]{1,0:T(8,128)(2,1)S(1)}, bf16[96,1536]{1,0:T(8,128)(2,1)S(1)}, u32[]{:S(2)}, u32[]{:S(2)}) %collective-permute-start.23) | collective-permute-done | bytes 294944 | tf_op jit(solution)/shard_map/ppermute | solution.py:77
  45.8 15.8 %collective-permute-done.22.refs_2_ = bf16[96,1536]{1,0:T(8,128)(2,1)S(1)} collective-permute-done((bf16[96,1536]{1,0:T(8,128)(2,1)S(1)}, bf16[96,1536]{1,0:T(8,128)(2,1)S(1)}, u32[]{:S(2)}, u32[]{:S(2)}) %collective-permute-start.22) | collective-permute-done | bytes 294944 | tf_op jit(solution)/shard_map/ppermute | solution.py:77
  69.4 9.4 %collective-permute-done.1.refs_2_ = bf16[112,768]{1,0:T(8,128)(2,1)S(1)} collective-permute-done((bf16[112,768]{1,0:T(8,128)(2,1)S(1)}, bf16[112,768]{1,0:T(8,128)(2,1)S(1)}, u32[]{:S(2)}, u32[]{:S(2)}) %collective-permute-start.1) | collective-permute-done | bytes 172064 | tf_op jit(solution)/shard_map/ppermute | solution.py:77
  82.8 18.9 %collective-permute-done.3.other = bf16[4,112,768]{2,1,0:T(8,128)(2,1)S(1)} collective-permute-done((bf16[4,112,768]{2,1,0:T(8,128)(2,1)S(1)}, bf16[4,112,768]{2,1,0:T(8,128)(2,1)S(1)}, u32[]{:S(2)}, u32[]{:S(2)}) %collective-permute-start.3) | collective-permute-done | bytes 688160 | tf_op jit(solution)/shard_map/ppermute | solution.py:74
  112.9 11.5 %collective-permute-done.5.to = bf16[768,384]{1,0:T(8,128)(2,1)} collective-permute-done((bf16[768,384]{1,0:T(8,128)(2,1)}, bf16[768,384]{1,0:T(8,128)(2,1)}, u32[]{:S(2)}, u32[]{:S(2)}) %collective-permute-start.5) | collective-permute-done | bytes 589856 | tf_op jit(solution)/shard_map/ppermute | solution.py:68
  132.1 8.5 %keyval.3 = (bf16[1280,768]{1,0:T(8,128)(2,1)S(1)}, bf16[1280,1536]{1,0:T(8,128)(2,1)}, bf16[768,1536]{1,0:T(8,128)(2,1)S(1)}, bf16[768,768]{1,0:T(8,128)(2,1)S(...) custom-call(s32[4]{0:T(128)S(1)} %pad_add_fusion.at, bf16[1280,768]{1,0:T(8,128)(2,1)S(1)} %bitcast.50, ...), custom_call_target="tpu_custom_call" | custom-call | flops 3170893824 | bytes 15556624 | tf_op jit(solution)/shard_map/keyval/pallas_call | solution.py:588
  145.5 6.9 %cross_fwd.1 = (bf16[128,768]{1,0:T(8,128)(2,1)S(1)}, f32[6,256,1]{2,1,0:T(8,128)S(1)}) custom-call(s32[1,1280]{1,0:T(1,128)S(1)} %copy-done.75, s32[1,128]{1,0:T(1,128)S(1)} %copy-done.82, bf16[128,768]{1,0:T(8,128)(2,1)S(1)} %get-tuple-element.115.q.refs_2_, bf16[1280,1536]{1,0:T(8,128)(2,1)S(1)} %copy-done, bf16[1280,1536]{1,0:T(8,128)(2,1)S(1)} %copy-done), custom_call_target="tpu_custom_call" | custom-call | flops 1006632960 | bytes 8269312 | tf_op jit(solution)/shard_map/cross_fwd/pallas_call | solution.py:588
  182.3 5.4 %ffn_first.1 = (f32[128,768]{1,0:T(8,128)S(1)}, f32[128,768]{1,0:T(8,128)S(1)}, f32[128,768]{1,0:T(8,128)S(1)}, f32[128,768]{1,0:T(8,128)S(1)}, bf16[768,1536]{1,0:T(8,128)(2,1)}) custom-call(s32[4]{0:T(128)S(1)} %pad_add_fusion.at, bf16[128,768]{1,0:T(8,128)(2,1)S(1)} %get-tuple-element.130.third0, bf16[128,768]{1,0:T(8,128)(2,1)S(1)} %collective-permute-done.19.third1, ...), custom_call_target="tpu_custom_call" | custom-call | flops 1811939328 | bytes 7077888 | tf_op jit(solution)/shard_map/ffn_first/pallas_call | solution.py:40
  187.7 3.9 ffn_second.1
  203.4 5.5 %self_back.1 = (f32[128,768]{1,0:T(8,128)S(1)}, bf16[128,768]{1,0:T(8,128)(2,1)S(1)}, bf16[768,576]{1,0:T(8,128)(2,1)S(1)}, bf16[768,576]{1,0:T(8,128)(2,1)S(1)}) custom-call(s32[4]{0:T(128)S(1)} %pad_add_fusion.at, bf16[256,1152]{1,0:T(8,128)(2,1)S(1)} %get-tuple-element.142.triple, bf16[128,384]{1,0:T(8,128)(2,1)S(1)} %get-tuple-element.143.da0, ...), custom_call_target="tpu_custom_call" | custom-call | flops 1207959552 | bytes 5309440 | tf_op jit(solution)/shard_map/self_back/pallas_call | solution.py:40
  221.4 5.9 %collective-permute-start.39 = (bf16[2,8,96,768]{3,2,1,0:T(8,128)(2,1)S(1)}, bf16[2,8,96,768]{3,2,1,0:T(8,128)(2,1)S(1)}, u32[]{:S(2)}, u32[]{:S(2)}) collective-permute-start(bf16[2,8,96,768]{3,2,1,0:T(8,128)(2,1)S(1)} %get-tuple-element.177), channel_id=1, source_target_pairs={{0,8},{8,0},{16,24},{24,16},{1,9},{9,1},{17,25},{25,17},{2,10},{10... | collective-permute-start | bytes 7077896 | tf_op jit(solution)/shard_map/ppermute | solution.py:65
  227.4 5.8 %cross_back.3 = (bf16[128,384]{1,0:T(8,128)(2,1)S(1)}, bf16[2,1280,384]{2,1,0:T(8,128)(2,1)S(1)}) custom-call(s32[4]{0:T(128)S(1)} %pad_add_fusion.at, s32[1,1280]{1,0:T(1,128)S(1)} %copy-done.76, s32[1,128]{1,0:T(1,128)S(1)} %copy-done.83, bf16[128,768]{1,0:T(8,128)(2,1)S(1)} %copy-done.23, bf16[1280,1536]{1,0:T(8,128)(2,1)S(1)} %copy-done.1, ...), custom_call_target="tpu_custom_call" | custom-call | flops 1258291200 | bytes 10333712 | tf_op jit(solution)/shard_map/cross_back/pallas_call | solution.py:669
  233.2 4.2 %cross_weights.3 = bf16[3,768,384]{2,1,0:T(8,128)(2,1)} custom-call(s32[4]{0:T(128)S(1)} %pad_add_fusion.at, bf16[1280,768]{1,0:T(8,128)(2,1)S(1)} %copy-done.4, bf16[128,768]{1,0:T(8,128)(2,1)S(1)} %copy-done.13, bf16[128,384]{1,0:T(8,128)(2,1)S(1)} %get-tuple-element.154.dq_oth.dq, bf16[2,1280,384]{2,1,0:T(8,128)(2,1)S(1)} %get-tuple-element.159.oth.dkv), custom_call_target="tpu_custom_call" | custom-call | flops 1509949440 | bytes 5996544 | tf_op jit(solution)/shard_map/cross_weights/pallas_call | solution.py:40
  246.9 5.8 %cross_back.2 = (bf16[128,384]{1,0:T(8,128)(2,1)S(1)}, bf16[2,1280,384]{2,1,0:T(8,128)(2,1)S(1)}) custom-call(s32[4]{0:T(128)S(1)} %pad_add_fusion.at, s32[1,1280]{1,0:T(1,128)S(1)} %copy-done.77, s32[1,128]{1,0:T(1,128)S(1)} %copy-done.84, bf16[128,768]{1,0:T(8,128)(2,1)S(1)} %copy-done.23, bf16[1280,1536]{1,0:T(8,128)(2,1)S(1)} %copy-done.2, ...), custom_call_target="tpu_custom_call" | custom-call | flops 1258291200 | bytes 10333712 | tf_op jit(solution)/shard_map/cross_back/pallas_call | solution.py:669
  267.2 14.3 %collective-permute-done.31.came = bf16[768,384]{1,0:T(8,128)(2,1)} collective-permute-done((bf16[768,384]{1,0:T(8,128)(2,1)}, bf16[768,384]{1,0:T(8,128)(2,1)}, u32[]{:S(2)}, u32[]{:S(2)}) %collective-permute-start.31) | collective-permute-done | bytes 589856 | tf_op jit(solution)/shard_map/ppermute | solution.py:68
  288.6 8.4 %text_back.1 = (f32[1280,768]{1,0:T(8,128)}, f32[2,768]{1,0:T(2,128)S(1)}) custom-call(s32[4]{0:T(128)S(1)} %pad_add_fusion.at, bf16[1280,768]{1,0:T(8,128)(2,1)S(1)} %bitcast.51, f32[1,3072]{1,0:T(1,128)S(1)} %get-tuple-element.111.gains, bf16[768,1536]{1,0:T(8,128)(2,1)S(1)} %copy-done.94, bf16[2,1280,384]{2,1,0:T(8,128)(2,1)S(1)} %copy-done.21, ...), custom_call_target="tpu_custom_call" | custom-call | flops 3019898880 | bytes 12208144 | tf_op jit(solution)/shard_map/text_back/pallas_call | solution.py:588
  303.5 4.4 %collective-permute-done.65 = f32[8,768]{1,0:T(8,128)S(1)} collective-permute-done((f32[8,768]{1,0:T(8,128)S(1)}, f32[8,768]{1,0:T(8,128)S(1)}, u32[]{:S(2)}, u32[]{:S(2)}) %collective-permute-start.65) | collective-permute-done | bytes 24608 | tf_op jit(solution)/shard_map/ppermute | solution.py:71
  309.9 11.6 %collective-permute-done.66 = f32[8,768]{1,0:T(8,128)S(1)} collective-permute-done((f32[8,768]{1,0:T(8,128)S(1)}, f32[8,768]{1,0:T(8,128)S(1)}, u32[]{:S(2)}, u32[]{:S(2)}) %collective-permute-start.66) | collective-permute-done | bytes 24608 | tf_op jit(solution)/shard_map/ppermute | solution.py:74
  323.0 6.5 %collective-permute-done.67 = f32[8,768]{1,0:T(8,128)S(1)} collective-permute-done((f32[8,768]{1,0:T(8,128)S(1)}, f32[8,768]{1,0:T(8,128)S(1)}, u32[]{:S(2)}, u32[]{:S(2)}) %collective-permute-start.67) | collective-permute-done | bytes 24608 | tf_op jit(solution)/shard_map/ppermute | solution.py:77
  333.1 30.4 %collective-permute-done.51.refs_2_ = bf16[96,576]{1,0:T(8,128)(2,1)S(1)} collective-permute-done((bf16[96,576]{1,0:T(8,128)(2,1)S(1)}, bf16[96,576]{1,0:T(8,128)(2,1)S(1)}, u32[]{:S(2)}, u32[]{:S(2)}) %collective-permute-start.51) | collective-permute-done | bytes 110624 | tf_op jit(solution)/shard_map/ppermute | solution.py:77
  384.3 9.4 %collective-permute-done.43.refs_2_ = bf16[96,768]{1,0:T(8,128)(2,1)S(1)} collective-permute-done((bf16[96,768]{1,0:T(8,128)(2,1)S(1)}, bf16[96,768]{1,0:T(8,128)(2,1)S(1)}, u32[]{:S(2)}, u32[]{:S(2)}) %collective-permute-start.43) | collective-permute-done | bytes 147488 | tf_op jit(solution)/shard_map/ppermute | solution.py:77
  (372 shorter events, 188.6 us)
Async XLA Ops:
  12.4 22.6 %collective-permute-start.9 = (bf16[96,1344]{1,0:T(8,128)(2,1)S(1)}, bf16[96,1344]{1,0:T(8,128)(2,1)S(1)}, u32[]{:S(2)}, u32[]{:S(2)}) collective-permute-start(bf16[96,1344]{1,0:T(8,128)(2,1)S(1)} %get-tuple-element.119.refs_0_), channel_id=1, source_target_pairs={{0,4},{1,5},{2,6},{3,7},{4,0},{5,1},{6,2},{7,3},{8,12},{9,13},{10,... | collective-permute-start | bytes 774152 | tf_op jit(solution)/shard_map/ppermute | solution.py:77
  12.4 22.6 %collective-permute-start.8 = (bf16[96,1344]{1,0:T(8,128)(2,1)S(1)}, bf16[96,1344]{1,0:T(8,128)(2,1)S(1)}, u32[]{:S(2)}, u32[]{:S(2)}) collective-permute-start(bf16[96,1344]{1,0:T(8,128)(2,1)S(1)} %get-tuple-element.119.refs_0_), channel_id=1, source_target_pairs={{0,2},{1,3},{2,0},{3,1},{4,6},{5,7},{6,4},{7,5},{8,10},{9,11},{10,... | collective-permute-start | bytes 774152 | tf_op jit(solution)/shard_map/ppermute | solution.py:77
  35.7 45.1 %collective-permute-start.11 = (bf16[4,96,1344]{2,1,0:T(8,128)(2,1)S(1)}, bf16[4,96,1344]{2,1,0:T(8,128)(2,1)S(1)}, u32[]{:S(2)}, u32[]{:S(2)}) collective-permute-start(bf16[4,96,1344]{2,1,0:T(8,128)(2,1)S(1)} %column.4.mine), channel_id=1, source_target_pairs={{0,1},{1,0},{2,3},{3,2},{4,5},{5,4},{6,7},{7,6},{8,9},{9,8},{10,11... | collective-permute-start | bytes 3096584 | tf_op jit(solution)/shard_map/ppermute | solution.py:74
  39.0 22.5 %collective-permute-start.22 = (bf16[96,1536]{1,0:T(8,128)(2,1)S(1)}, bf16[96,1536]{1,0:T(8,128)(2,1)S(1)}, u32[]{:S(2)}, u32[]{:S(2)}) collective-permute-start(bf16[96,1536]{1,0:T(8,128)(2,1)S(1)} %get-tuple-element.131.refs_0_), channel_id=1, source_target_pairs={{0,4},{1,5},{2,6},{3,7},{4,0},{5,1},{6,2},{7,3},{8,12},{9,13},{10,... | collective-permute-start | bytes 884744 | tf_op jit(solution)/shard_map/ppermute | solution.py:77
  62.2 45.3 %collective-permute-start.24 = (bf16[4,96,1536]{2,1,0:T(8,128)(2,1)S(1)}, bf16[4,96,1536]{2,1,0:T(8,128)(2,1)S(1)}, u32[]{:S(2)}, u32[]{:S(2)}) collective-permute-start(bf16[4,96,1536]{2,1,0:T(8,128)(2,1)S(1)} %column.5.mine), channel_id=1, source_target_pairs={{0,1},{1,0},{2,3},{3,2},{4,5},{5,4},{6,7},{7,6},{8,9},{9,8},{10,11... | collective-permute-start | bytes 3538952 | tf_op jit(solution)/shard_map/ppermute | solution.py:74
  81.5 31.0 %collective-permute-start.13 = (bf16[8,96,768]{2,1,0:T(8,128)(2,1)S(1)}, bf16[8,96,768]{2,1,0:T(8,128)(2,1)S(1)}, u32[]{:S(2)}, u32[]{:S(2)}) collective-permute-start(bf16[8,96,768]{2,1,0:T(8,128)(2,1)S(1)} %bitcast.38), channel_id=1, source_target_pairs={{0,16},{8,24},{16,0},{24,8},{1,17},{9,25},{17,1},{25,9},{2,18},{10... | collective-permute-start | bytes 3538952 | tf_op jit(solution)/shard_map/ppermute | solution.py:68
  109.6 69.2 %collective-permute-start.25 = (bf16[768,1536]{1,0:T(8,128)(2,1)}, bf16[768,1536]{1,0:T(8,128)(2,1)}, u32[]{:S(2)}, u32[]{:S(2)}) collective-permute-start(bf16[768,1536]{1,0:T(8,128)(2,1)} %bitcast.14.w), channel_id=1, source_target_pairs={{0,8},{8,0},{16,24},{24,16},{1,9},{9,1},{17,25},{25,17},{2,10},{10... | collective-permute-start | bytes 7077896 | tf_op jit(solution)/shard_map/ppermute | solution.py:65
  112.4 40.0 %collective-permute-start.12 = (bf16[8,96,768]{2,1,0:T(8,128)(2,1)S(1)}, bf16[8,96,768]{2,1,0:T(8,128)(2,1)}, u32[]{:S(2)}, u32[]{:S(2)}) collective-permute-start(bf16[8,96,768]{2,1,0:T(8,128)(2,1)S(1)} %bitcast.39), channel_id=1, source_target_pairs={{0,8},{8,0},{16,24},{24,16},{1,9},{9,1},{17,25},{25,17},{2,10},{10... | collective-permute-start | bytes 3538952 | tf_op jit(solution)/shard_map/ppermute | solution.py:65
  112.4 40.0 %collective-permute-start.14 = (bf16[8,96,768]{2,1,0:T(8,128)(2,1)S(1)}, bf16[8,96,768]{2,1,0:T(8,128)(2,1)}, u32[]{:S(2)}, u32[]{:S(2)}) collective-permute-start(bf16[8,96,768]{2,1,0:T(8,128)(2,1)S(1)} %collective-permute-done.13.to), channel_id=1, source_target_pairs={{0,8},{8,0},{16,24},{24,16},{1,9},{9,1},{17,25},{25,17},{2,10},{10... | collective-permute-start | bytes 3538952 | tf_op jit(solution)/shard_map/ppermute | solution.py:65
  127.0 34.5 %collective-permute-start.17 = (bf16[768,576]{0,1:T(8,128)(2,1)}, bf16[768,576]{0,1:T(8,128)(2,1)}, u32[]{:S(2)}, u32[]{:S(2)}) collective-permute-start(bf16[768,576]{0,1:T(8,128)(2,1)} %copy.28), channel_id=1, source_target_pairs={{0,8},{8,0},{16,24},{24,16},{1,9},{9,1},{17,25},{25,17},{2,10},{10... | collective-permute-start | bytes 2654216 | tf_op jit(solution)/shard_map/ppermute | solution.py:65
  227.4 25.3 %collective-permute-start.56 = (bf16[768,1536]{1,0:T(8,128)(2,1)}, bf16[768,1536]{1,0:T(8,128)(2,1)}, u32[]{:S(2)}, u32[]{:S(2)}) collective-permute-start(bf16[768,1536]{1,0:T(8,128)(2,1)} %get-tuple-element.195), channel_id=1, source_target_pairs={{0,8},{8,0},{16,24},{24,16},{1,9},{9,1},{17,25},{25,17},{2,10},{10... | collective-permute-start | bytes 7077896 | tf_op jit(solution)/shard_map/ppermute | solution.py:65
  237.4 23.4 %collective-permute-start.30 = (bf16[3,768,384]{2,1,0:T(8,128)(2,1)}, bf16[3,768,384]{2,1,0:T(8,128)(2,1)}, u32[]{:S(2)}, u32[]{:S(2)}) collective-permute-start(bf16[3,768,384]{2,1,0:T(8,128)(2,1)} %cross_weights.3), channel_id=1, source_target_pairs={{0,8},{8,0},{16,24},{24,16},{1,9},{9,1},{17,25},{25,17},{2,10},{10... | collective-permute-start | bytes 5308424 | tf_op jit(solution)/shard_map/ppermute | solution.py:65
  241.0 42.9 %collective-permute-start.40 = (bf16[8,96,768]{2,1,0:T(8,128)(2,1)}, bf16[8,96,768]{2,1,0:T(8,128)(2,1)}, u32[]{:S(2)}, u32[]{:S(2)}) collective-permute-start(bf16[8,96,768]{2,1,0:T(8,128)(2,1)} %get-tuple-element.179), channel_id=1, source_target_pairs={{0,16},{8,24},{16,0},{24,8},{1,17},{9,25},{17,1},{25,9},{2,18},{10... | collective-permute-start | bytes 3538952 | tf_op jit(solution)/shard_map/ppermute | solution.py:68
  257.6 50.4 %collective-permute-start.57 = (bf16[4,96,1536]{2,1,0:T(8,128)(2,1)}, bf16[4,96,1536]{2,1,0:T(8,128)(2,1)}, u32[]{:S(2)}, u32[]{:S(2)}) collective-permute-start(bf16[4,96,1536]{2,1,0:T(8,128)(2,1)} %get-tuple-element.197), channel_id=1, source_target_pairs={{0,1},{1,0},{2,3},{3,2},{4,5},{5,4},{6,7},{7,6},{8,9},{9,8},{10,11... | collective-permute-start | bytes 3538952 | tf_op jit(solution)/shard_map/ppermute | solution.py:74
  265.9 36.7 %collective-permute-start.49 = (bf16[4,96,576]{2,1,0:T(8,128)(2,1)S(1)}, bf16[4,96,576]{2,1,0:T(8,128)(2,1)S(1)}, u32[]{:S(2)}, u32[]{:S(2)}) collective-permute-start(bf16[4,96,576]{2,1,0:T(8,128)(2,1)S(1)} %get-tuple-element.189), channel_id=1, source_target_pairs={{0,1},{1,0},{2,3},{3,2},{4,5},{5,4},{6,7},{7,6},{8,9},{9,8},{10,11... | collective-permute-start | bytes 1327112 | tf_op jit(solution)/shard_map/ppermute | solution.py:74
  283.5 48.4 %collective-permute-start.32 = (bf16[4,96,768]{2,1,0:T(8,128)(2,1)S(1)}, bf16[4,96,768]{2,1,0:T(8,128)(2,1)S(1)}, u32[]{:S(2)}, u32[]{:S(2)}) collective-permute-start(bf16[4,96,768]{2,1,0:T(8,128)(2,1)S(1)} %get-tuple-element.169), channel_id=1, source_target_pairs={{0,1},{1,0},{2,3},{3,2},{4,5},{5,4},{6,7},{7,6},{8,9},{9,8},{10,11... | collective-permute-start | bytes 1769480 | tf_op jit(solution)/shard_map/ppermute | solution.py:74
  285.9 79.4 %collective-permute-start.41 = (bf16[4,96,768]{2,1,0:T(8,128)(2,1)S(1)}, bf16[4,96,768]{2,1,0:T(8,128)(2,1)S(1)}, u32[]{:S(2)}, u32[]{:S(2)}) collective-permute-start(bf16[4,96,768]{2,1,0:T(8,128)(2,1)S(1)} %get-tuple-element.181), channel_id=1, source_target_pairs={{0,1},{1,0},{2,3},{3,2},{4,5},{5,4},{6,7},{7,6},{8,9},{9,8},{10,11... | collective-permute-start | bytes 1769480 | tf_op jit(solution)/shard_map/ppermute | solution.py:74
  321.5 42.0 %collective-permute-start.58 = (bf16[96,1536]{1,0:T(8,128)(2,1)S(1)}, bf16[96,1536]{1,0:T(8,128)(2,1)S(1)}, u32[]{:S(2)}, u32[]{:S(2)}) collective-permute-start(bf16[96,1536]{1,0:T(8,128)(2,1)S(1)} %get-tuple-element.199), channel_id=1, source_target_pairs={{0,2},{1,3},{2,0},{3,1},{4,6},{5,7},{6,4},{7,5},{8,10},{9,11},{10,... | collective-permute-start | bytes 884744 | tf_op jit(solution)/shard_map/ppermute | solution.py:77
  329.5 38.3 %collective-permute-start.59 = (bf16[96,1536]{1,0:T(8,128)(2,1)S(1)}, bf16[96,1536]{1,0:T(8,128)(2,1)S(1)}, u32[]{:S(2)}, u32[]{:S(2)}) collective-permute-start(bf16[96,1536]{1,0:T(8,128)(2,1)S(1)} %get-tuple-element.200), channel_id=1, source_target_pairs={{0,4},{1,5},{2,6},{3,7},{4,0},{5,1},{6,2},{7,3},{8,12},{9,13},{10,... | collective-permute-start | bytes 884744 | tf_op jit(solution)/shard_map/ppermute | solution.py:77
  330.1 39.2 %collective-permute-start.60 = (bf16[96,1536]{1,0:T(8,128)(2,1)S(1)}, bf16[96,1536]{1,0:T(8,128)(2,1)S(1)}, u32[]{:S(2)}, u32[]{:S(2)}) collective-permute-start(bf16[96,1536]{1,0:T(8,128)(2,1)S(1)} %get-tuple-element.201), channel_id=1, source_target_pairs={{0,6},{1,7},{2,4},{3,5},{4,2},{5,3},{6,0},{7,1},{8,14},{9,15},{10,... | collective-permute-start | bytes 884744 | tf_op jit(solution)/shard_map/ppermute | solution.py:77
  331.9 31.6 %collective-permute-start.51 = (bf16[96,576]{1,0:T(8,128)(2,1)S(1)}, bf16[96,576]{1,0:T(8,128)(2,1)S(1)}, u32[]{:S(2)}, u32[]{:S(2)}) collective-permute-start(bf16[96,576]{1,0:T(8,128)(2,1)S(1)} %get-tuple-element.192), channel_id=1, source_target_pairs={{0,4},{1,5},{2,6},{3,7},{4,0},{5,1},{6,2},{7,3},{8,12},{9,13},{10,... | collective-permute-start | bytes 331784 | tf_op jit(solution)/shard_map/ppermute | solution.py:77
  370.7 31.0 %collective-permute-start.61 = (bf16[96,1536]{1,0:T(8,128)(2,1)S(1)}, bf16[96,1536]{1,0:T(8,128)(2,1)S(1)}, u32[]{:S(2)}, u32[]{:S(2)}) collective-permute-start(bf16[96,1536]{1,0:T(8,128)(2,1)S(1)} %reduce_sum.7.refs_8_), channel_id=1, source_target_pairs={{0,16},{8,24},{16,0},{24,8},{1,17},{9,25},{17,1},{25,9},{2,18},{10... | collective-permute-start | bytes 884744 | tf_op jit(solution)/shard_map/ppermute | solution.py:68
  370.9 22.8 %collective-permute-start.43 = (bf16[96,768]{1,0:T(8,128)(2,1)S(1)}, bf16[96,768]{1,0:T(8,128)(2,1)S(1)}, u32[]{:S(2)}, u32[]{:S(2)}) collective-permute-start(bf16[96,768]{1,0:T(8,128)(2,1)S(1)} %get-tuple-element.184), channel_id=1, source_target_pairs={{0,4},{1,5},{2,6},{3,7},{4,0},{5,1},{6,2},{7,3},{8,12},{9,13},{10,... | collective-permute-start | bytes 442376 | tf_op jit(solution)/shard_map/ppermute | solution.py:77
  377.7 23.0 %collective-permute-start.36 = (bf16[96,768]{1,0:T(8,128)(2,1)S(1)}, bf16[96,768]{1,0:T(8,128)(2,1)S(1)}, u32[]{:S(2)}, u32[]{:S(2)}) collective-permute-start(bf16[96,768]{1,0:T(8,128)(2,1)S(1)} %reduce_sum.4.r), channel_id=1, source_target_pairs={{0,16},{8,24},{16,0},{24,8},{1,17},{9,25},{17,1},{25,9},{2,18},{10... | collective-permute-start | bytes 442376 | tf_op jit(solution)/shard_map/ppermute | solution.py:68
  (145 other events, 1245.6 us)
